TPU v7x, 32 devices: a whole 2x2x4 slice. The times are simulated.
32 devices in a mesh: gx: 8 (over y, x, core), gy: 4 (over z).
Axes of the slice: x: 2, y: 2, z: 4, core: 2. Of those that a mesh axis runs over, the one named last changes fastest.
Arguments:
- features: bfloat16 [8, 4, 512, 128], P('gx', 'gy'), may hold values from -6 to 6
- cotangent: bfloat16 [8, 4, 512, 128], P('gx', 'gy'), may hold values from -6 to 6
- weight_one: bfloat16 [27, 128, 128], replicated, may hold values from -0.125 to 0.125
- weight_two: bfloat16 [27, 128, 128], replicated, may hold values from -0.125 to 0.125
- block_count: int32 [8, 4], P('gx', 'gy'), may hold values from 4 to 8, as said below
- send_list: int32 [8, 4, 8, 4], P('gx', 'gy'), may hold values from 0 to 7, as said below
- rulebook: int32 [8, 4, 27, 512], P('gx', 'gy'), may hold values from 0 to 2560, as said below
Outputs:
- output: bfloat16 [8, 4, 512, 128], P('gx', 'gy')
- grad_features: bfloat16 [8, 4, 512, 128], P('gx', 'gy')
- grad_one: float32 [27, 128, 128], P(None, 'gx')
- grad_two: float32 [27, 128, 128], P(None, 'gx')
Inputs may be any that keep to these rules, and one draw needn't show every extreme that they name: The active blocks of a device are its first block_count blocks; some device has 8. send_list[a, b, e] lists the 4 blocks that device (a, b) sends toward the device at direction d_e; every entry is an active block of the sender; entries may repeat. rulebook[a, b, k, i] is a row of device (a, b)'s extended table; 2560 is the zero row and means no neighbour at that offset. Rows of inactive blocks hold 2560 at every offset; for an active row, offset 13 is the row itself; every other entry below 2560 is an active row of the device or a row of the slot of a neighbouring device that exists.
All inputs are finite; a program needn't handle non-finite values.
Results may differ from a plain program's by a relative error of at most 0.0055.
Values may be sent and summed in bfloat16 or wider, within the bound.
A program may use at most 128 MiB of HBM per device.

v0:
```python
import jax
import jax.numpy as jnp
from jax import lax
from jax.sharding import PartitionSpec as P

BLK = 64


DIRECTIONS = ((-1, -1), (-1, 0), (-1, 1), (0, -1), (0, 1), (1, -1), (1, 0), (1, 1))


def shifted(block, axis, distance):
    devices = range(lax.axis_size(axis))
    route = [(i - distance, i) for i in devices if i - distance in devices]
    return lax.ppermute(block, axis, route)


def deliver(buffers):
    arrived = []
    for index_e, (step_x, step_y) in enumerate(DIRECTIONS):
        moving = buffers[index_e]
        if step_x != 0:
            moving = shifted(moving, "gx", step_x)
        if step_y != 0:
            moving = shifted(moving, "gy", step_y)
        arrived.append(moving)
    return jnp.stack(arrived, 0)


def block_plan(row_total):
    block_span = min(512, row_total)
    return (block_span, row_total // block_span)


def extend_field(field, send_blocks):
    row_total, channels = field.shape
    block_rows = field.reshape(row_total // BLK, BLK, channels)
    outgoing = block_rows[send_blocks.reshape(-1)].reshape(8, -1, channels)
    arrived = deliver(outgoing)
    halo_rows = arrived[::-1].reshape(-1, channels)
    return jnp.concatenate((field, halo_rows, jnp.zeros((1, channels), field.dtype)), 0)


def conv_forward(extended, rule_rows, weight):
    row_total, kernel = rule_rows.shape
    block_span, blocks = block_plan(row_total)
    channels = weight.shape[1]
    stacked = weight.reshape(kernel * channels, -1)

    def one_block(indices):
        gathered = extended[indices].reshape(block_span, kernel * channels)
        return jnp.dot(gathered, stacked, preferred_element_type=jnp.float32)

    results = lax.map(one_block, rule_rows.reshape(blocks, block_span, kernel))
    return results.reshape(row_total, -1)


def conv_transpose(grads, rule_rows, weight, send_blocks, table_rows):
    row_total, channels = grads.shape
    kernel = rule_rows.shape[1]
    block_span, blocks = block_plan(row_total)
    flipped = jnp.transpose(weight, (2, 0, 1)).reshape(channels, kernel * channels)

    def conv_add_block(totals, item):
        indices, pieces = item
        terms = jnp.dot(pieces, flipped, preferred_element_type=jnp.float32).reshape(
            block_span * kernel, channels
        )
        return (totals.at[indices.reshape(-1)].add(terms), None)

    start = jnp.zeros((table_rows, channels), jnp.float32)
    totals, ignored = lax.scan(
        conv_add_block,
        start,
        (
            rule_rows.reshape(blocks, block_span, kernel),
            grads.reshape(blocks, block_span, channels),
        ),
    )
    halo_part = totals[row_total : table_rows - 1].astype(jnp.bfloat16).reshape(8, -1, channels)
    returned = deliver(halo_part).astype(jnp.float32)
    local_blocks = totals[:row_total].reshape(row_total // BLK, BLK, channels)
    targets = send_blocks[::-1].reshape(-1)
    local_blocks = local_blocks.at[targets].add(returned.reshape(targets.shape[0], BLK, channels))
    return local_blocks.reshape(row_total, channels)


def weight_grad(extended, rule_rows, grads):
    row_total, kernel = rule_rows.shape
    channels = extended.shape[1]
    block_span, blocks = block_plan(row_total)

    def weight_add_block(totals, item):
        indices, pieces = item
        gathered = extended[indices].reshape(block_span, kernel * channels)
        product = lax.dot_general(
            gathered, pieces, (((0,), (0,)), ((), ())), preferred_element_type=jnp.float32
        )
        return (totals + product, None)

    start = jnp.zeros((kernel * channels, grads.shape[1]), jnp.float32)
    totals, ignored = lax.scan(
        weight_add_block,
        start,
        (rule_rows.reshape(blocks, block_span, kernel), grads.reshape(blocks, block_span, -1)),
    )
    return totals.reshape(kernel, channels, -1)


def on_device(features, cotangent, weight_one, weight_two, block_count, send_list, rulebook):
    field = features[0, 0]
    send_blocks = send_list[0, 0]
    rule_rows = rulebook[0, 0].T
    row_total, channels = field.shape
    table_rows = row_total + send_blocks.size * BLK + 1
    live_rows = (
        lax.broadcasted_iota(jnp.int32, (row_total, 1), 0) // BLK < block_count[0, 0]
    ).astype(jnp.float32)
    live_half = live_rows.astype(jnp.bfloat16)
    masked = field * live_half
    ext_input = extend_field(masked, send_blocks)
    first_pre = conv_forward(ext_input, rule_rows, weight_one) * live_rows
    hidden = jax.nn.silu(first_pre).astype(jnp.bfloat16)
    ext_hidden = extend_field(hidden, send_blocks)
    output = (conv_forward(ext_hidden, rule_rows, weight_two) * live_rows).astype(jnp.bfloat16)
    upstream = cotangent[0, 0] * live_half
    grad_hidden = conv_transpose(upstream, rule_rows, weight_two, send_blocks, table_rows)
    partial_two = weight_grad(ext_hidden, rule_rows, upstream)
    sigmoid_pre = jax.nn.sigmoid(first_pre)
    grad_pre = (
        grad_hidden * sigmoid_pre * (1.0 + first_pre * (1.0 - sigmoid_pre)) * live_rows
    ).astype(jnp.bfloat16)
    partial_one = weight_grad(ext_input, rule_rows, grad_pre)
    grad_input = (
        conv_transpose(grad_pre, rule_rows, weight_one, send_blocks, table_rows) * live_rows
    ).astype(jnp.bfloat16)
    device_total = lax.axis_size("gx") * lax.axis_size("gy")
    slab_one, slab_two = (
        lax.psum_scatter(partial_one, "gx", scatter_dimension=1, tiled=True),
        lax.psum_scatter(partial_two, "gx", scatter_dimension=1, tiled=True),
    )
    summed_one, summed_two = lax.psum((slab_one, slab_two), "gy")
    return (
        output[None, None],
        grad_input[None, None],
        summed_one / device_total,
        summed_two / device_total,
    )


def solution(mesh):
    placed = (
        P("gx", "gy", None, None),
        P("gx", "gy", None, None),
        P(),
        P(),
        P("gx", "gy"),
        P("gx", "gy", None, None),
        P("gx", "gy", None, None),
    )
    return jax.shard_map(
        on_device,
        mesh=mesh,
        in_specs=placed,
        out_specs=(
            P("gx", "gy", None, None),
            P("gx", "gy", None, None),
            P(None, "gx", None),
            P(None, "gx", None),
        ),
        check_vma=False,
    )
```

profile of v0, /device:TPU:0, one launch (start us, length us, event | category | flops | bytes accessed | tf_op | source)
XLA Modules:
  0.0 519.6 jit_solution(1594714296753103766)
XLA Ops:
  8.0 5.3 %fusion.22 = f32[512,3456]{1,0:T(8,128)} fusion(bf16[128,3456]{0,1:T(8,128)(2,1)} %bitcast.166, bf16[1,1,512,128]{3,2,1,0:T(8,128)(2,1)} %param.8, bf16[512]{0:T(512)(128)(2,1)S(1)} %fusion.38), kind=kOutput, calls=%fused_computation.32 | convolution fusion | flops 453050368 | bytes 8094720 | tf_op jit(solution)/shard_map/while/body/eval_jaxpr/dot_general | solution.py:66
  13.3 7.9 %reshape.446 = f32[13824,128]{1,0:T(8,128)} reshape(f32[512,3456]{1,0:T(8,128)} %fusion.22) | data formatting | bytes 14155776 | tf_op jit(solution)/shard_map/while/body/eval_jaxpr/reshape | solution.py:66
  21.8 74.4 %scatter_custom_fusion = f32[2561,128]{1,0:T(8,128)S(1)} fusion(s32[13824]{0:T(1024)S(1)} %fusion.28, f32[13824,128]{1,0:T(8,128)} %reshape.446, f32[]{:T(128)} %constant.101.clone.1), kind=kCustom, calls=%fused_computation.20 | custom fusion | flops 1769472 | bytes 1311744 | tf_op jit(solution)/shard_map/while/body/eval_jaxpr/scatter-add | solution.py:69
  112.0 13.8 %collective-permute-start.30 = (bf16[256,128]{1,0:T(8,128)(2,1)}, bf16[256,128]{1,0:T(8,128)(2,1)S(1)}, u32[]{:S(2)}, u32[]{:S(2)}) collective-permute-start(bf16[256,128]{1,0:T(8,128)(2,1)} %get-tuple-element.92), channel_id=1, source_target_pairs={{0,1},{1,2},{2,3},{4,5},{5,6},{6,7},{8,9},{9,10},{10,11},{12,13},{... | collective-permute-start | bytes 196616 | tf_op jit(solution)/shard_map/ppermute | solution.py:15
  127.3 4.8 collective-permute-done.1
  135.7 5.6 %collective-permute-start.33 = (bf16[256,128]{1,0:T(8,128)(2,1)}, bf16[256,128]{1,0:T(8,128)(2,1)S(1)}, u32[]{:S(2)}, u32[]{:S(2)}) collective-permute-start(bf16[256,128]{1,0:T(8,128)(2,1)} %get-tuple-element.90), channel_id=1, source_target_pairs={{0,4},{4,8},{8,12},{12,16},{16,20},{20,24},{24,28},{1,5},{5,9},{9,... | collective-permute-start | bytes 196616 | tf_op jit(solution)/shard_map/ppermute | solution.py:15
  141.3 4.1 collective-permute-start.28
  153.8 5.1 collective-permute-done.32
  160.2 4.5 collective-permute-start.6
  174.1 6.4 %collective-permute-start.10 = (bf16[256,128]{1,0:T(8,128)(2,1)S(1)}, bf16[256,128]{1,0:T(8,128)(2,1)S(1)}, u32[]{:S(2)}, u32[]{:S(2)}) collective-permute-start(bf16[256,128]{1,0:T(8,128)(2,1)S(1)} %bitcast.174), channel_id=1, source_target_pairs={{0,4},{4,8},{8,12},{12,16},{16,20},{20,24},{24,28},{1,5},{5,9},{9,... | collective-permute-start | bytes 196616 | tf_op jit(solution)/shard_map/ppermute | solution.py:15
  180.6 4.3 collective-permute-start.4
  187.8 4.5 collective-permute-start.11
  194.8 28.4 %gather_fusion.1 = bf16[13824,128]{1,0:T(8,128)(2,1)} fusion(bf16[2561,128]{1,0:T(8,128)(2,1)S(1)} %maximum_maximum_fusion, s32[14336]{0:T(1024)S(1)} %pad_clamp_fusion), kind=kCustom, calls=%fused_computation.1 | custom fusion | bytes 7133184 | tf_op jit(solution)/shard_map/while/body/eval_jaxpr/gather | solution.py:51
  223.1 6.6 %reshape.419 = bf16[512,27,128]{2,1,0:T(8,128)(2,1)} reshape(bf16[13824,128]{1,0:T(8,128)(2,1)} %gather_fusion.1) | data formatting | bytes 7077888 | tf_op jit(solution)/shard_map/while/body/eval_jaxpr/gather | solution.py:51
  237.6 7.5 %reshape.406 = bf16[512,3456]{1,0:T(8,128)(2,1)} reshape(bf16[13824,128]{1,0:T(8,128)(2,1)} %gather_fusion.1) | data formatting | bytes 7077888 | tf_op jit(solution)/shard_map/while/body/eval_jaxpr/reshape | solution.py:51
  245.1 5.7 %copy.23 = bf16[3456,512]{1,0:T(8,128)(2,1)} copy(bf16[3456,512]{0,1:T(8,128)(2,1)} %bitcast.154) | data formatting | bytes 7077888 | tf_op jit(solution)/shard_map/while/body/eval_jaxpr/dot_general | solution.py:96
  252.3 4.3 fusion.46
  260.6 5.6 %collective-permute-start.18 = (bf16[256,128]{1,0:T(8,128)(2,1)S(1)}, bf16[256,128]{1,0:T(8,128)(2,1)S(1)}, u32[]{:S(2)}, u32[]{:S(2)}) collective-permute-start(bf16[256,128]{1,0:T(8,128)(2,1)S(1)} %bitcast.179), channel_id=1, source_target_pairs={{0,1},{1,2},{2,3},{4,5},{5,6},{6,7},{8,9},{9,10},{10,11},{12,13},{... | collective-permute-start | bytes 196616 | tf_op jit(solution)/shard_map/ppermute | solution.py:15
  281.3 4.5 collective-permute-start.23
  288.2 28.4 %gather_fusion.3 = bf16[13824,128]{1,0:T(8,128)(2,1)} fusion(bf16[2561,128]{1,0:T(8,128)(2,1)S(1)} %maximum_maximum_fusion.1, s32[14336]{0:T(1024)S(1)} %pad_clamp_fusion), kind=kCustom, calls=%fused_computation.3 | custom fusion | bytes 7133184 | tf_op jit(solution)/shard_map/while/body/eval_jaxpr/gather | solution.py:51
  316.7 7.5 %reshape.407 = bf16[512,3456]{1,0:T(8,128)(2,1)} reshape(bf16[13824,128]{1,0:T(8,128)(2,1)} %gather_fusion.3) | data formatting | bytes 7077888 | tf_op jit(solution)/shard_map/while/body/eval_jaxpr/reshape | solution.py:51
  324.2 5.8 %copy.24 = bf16[3456,512]{1,0:T(8,128)(2,1)} copy(bf16[3456,512]{0,1:T(8,128)(2,1)} %bitcast.155) | data formatting | bytes 7077888 | tf_op jit(solution)/shard_map/while/body/eval_jaxpr/dot_general | solution.py:96
  330.0 4.4 fusion.20
  338.5 8.0 %reshape.462 = f32[13824,128]{1,0:T(8,128)} reshape(f32[512,3456]{1,0:T(8,128)} %fusion.45) | data formatting | bytes 14155776 | tf_op jit(solution)/shard_map/while/body/eval_jaxpr/reshape | solution.py:66
  346.5 74.4 %scatter_custom_fusion.2 = f32[2561,128]{1,0:T(8,128)S(1)} fusion(s32[13824]{0:T(1024)} %copy-done.7, f32[13824,128]{1,0:T(8,128)} %reshape.462, f32[]{:T(128)} %constant.101.clone.1), kind=kCustom, calls=%fused_computation.18 | custom fusion | flops 1769472 | bytes 1311744 | tf_op jit(solution)/shard_map/while/body/eval_jaxpr/scatter-add | solution.py:69
  422.3 6.4 %collective-permute-done.36 = bf16[256,128]{1,0:T(8,128)(2,1)S(1)} collective-permute-done((bf16[256,128]{1,0:T(8,128)(2,1)S(1)}, bf16[256,128]{1,0:T(8,128)(2,1)S(1)}, u32[]{:S(2)}, u32[]{:S(2)}) %collective-permute-start.36) | collective-permute-done | bytes 65568 | tf_op jit(solution)/shard_map/ppermute | solution.py:15
  433.9 12.0 %collective-permute-start.42 = (bf16[256,128]{1,0:T(8,128)(2,1)S(1)}, bf16[256,128]{1,0:T(8,128)(2,1)S(1)}, u32[]{:S(2)}, u32[]{:S(2)}) collective-permute-start(bf16[256,128]{1,0:T(8,128)(2,1)S(1)} %get-tuple-element.74), channel_id=1, source_target_pairs={{0,1},{1,2},{2,3},{4,5},{5,6},{6,7},{8,9},{9,10},{10,11},{12,13},{... | collective-permute-start | bytes 196616 | tf_op jit(solution)/shard_map/ppermute | solution.py:15
  453.2 4.7 collective-permute-start.40
  461.4 4.5 collective-permute-start.47
  471.0 6.7 %reshape.435 = bf16[512,27,128]{2,1,0:T(8,128)(2,1)} reshape(bf16[13824,128]{1,0:T(8,128)(2,1)} %gather_fusion.3) | data formatting | bytes 7077888 | tf_op jit(solution)/shard_map/while/body/eval_jaxpr/gather | solution.py:51
  477.7 4.1 fusion.13
  481.8 28.0 %all-reduce.3.cloned.1.call-done = (f32[27,16,128]{2,1,0:T(8,128)}, f32[27,16,128]{2,1,0:T(8,128)}) async-done(((f32[27,16,128]{2,1,0:T(8,128)}, f32[27,16,128]{2,1,0:T(8,128)}), (f32[27,16,128]{2,1,0:T(8,128)}, f32[27,16,128]{2,1,0:T(8,128)})) %all-reduce.3.cloned.1.call-update) | async-done | bytes 442384 | tf_op jit(solution)/shard_map/psum | solution.py:142
  (185 shorter events, 105.5 us)
Async XLA Ops:
  7.2 463.0 %reduce-scatter.3.cloned.1.call-start = ((), (), s32[]{:S(2)}) async-start(), calls=%async_computation.2 | async-start | bytes 1990656 | tf_op jit(solution)/shard_map/reduce_scatter | solution.py:139
  98.5 37.2 %collective-permute-start.26 = (bf16[256,128]{1,0:T(8,128)(2,1)}, bf16[256,128]{1,0:T(8,128)(2,1)}, u32[]{:S(2)}, u32[]{:S(2)}) collective-permute-start(bf16[256,128]{1,0:T(8,128)(2,1)} %get-tuple-element.100), channel_id=1, source_target_pairs={{4,0},{8,4},{12,8},{16,12},{20,16},{24,20},{28,24},{5,1},{9,5},{13... | collective-permute-start | bytes 196616 | tf_op jit(solution)/shard_map/ppermute | solution.py:15
  99.8 41.6 %collective-permute-start.27 = (bf16[256,128]{1,0:T(8,128)(2,1)}, bf16[256,128]{1,0:T(8,128)(2,1)}, u32[]{:S(2)}, u32[]{:S(2)}) collective-permute-start(bf16[256,128]{1,0:T(8,128)(2,1)} %get-tuple-element.94), channel_id=1, source_target_pairs={{4,0},{8,4},{12,8},{16,12},{20,16},{24,20},{28,24},{5,1},{9,5},{13... | collective-permute-start | bytes 196616 | tf_op jit(solution)/shard_map/ppermute | solution.py:15
  101.1 47.9 %collective-permute-start.29 = (bf16[256,128]{1,0:T(8,128)(2,1)}, bf16[256,128]{1,0:T(8,128)(2,1)}, u32[]{:S(2)}, u32[]{:S(2)}) collective-permute-start(bf16[256,128]{1,0:T(8,128)(2,1)} %get-tuple-element.93), channel_id=1, source_target_pairs={{1,0},{2,1},{3,2},{5,4},{6,5},{7,6},{9,8},{10,9},{11,10},{13,12},{... | collective-permute-start | bytes 196616 | tf_op jit(solution)/shard_map/ppermute | solution.py:15
  106.9 19.1 %collective-permute-start.25 = (bf16[256,128]{1,0:T(8,128)(2,1)}, bf16[256,128]{1,0:T(8,128)(2,1)S(1)}, u32[]{:S(2)}, u32[]{:S(2)}) collective-permute-start(bf16[256,128]{1,0:T(8,128)(2,1)} %collective-permute-done.24), channel_id=1, source_target_pairs={{1,0},{2,1},{3,2},{5,4},{6,5},{7,6},{9,8},{10,9},{11,10},{13,12},{... | collective-permute-start | bytes 196616 | tf_op jit(solution)/shard_map/ppermute | solution.py:15
  112.0 39.1 %collective-permute-start.30 = (bf16[256,128]{1,0:T(8,128)(2,1)}, bf16[256,128]{1,0:T(8,128)(2,1)S(1)}, u32[]{:S(2)}, u32[]{:S(2)}) collective-permute-start(bf16[256,128]{1,0:T(8,128)(2,1)} %get-tuple-element.92), channel_id=1, source_target_pairs={{0,1},{1,2},{2,3},{4,5},{5,6},{6,7},{8,9},{9,10},{10,11},{12,13},{... | collective-permute-start | bytes 196616 | tf_op jit(solution)/shard_map/ppermute | solution.py:15
  132.1 20.3 %collective-permute-start.31 = (bf16[256,128]{1,0:T(8,128)(2,1)}, bf16[256,128]{1,0:T(8,128)(2,1)S(1)}, u32[]{:S(2)}, u32[]{:S(2)}) collective-permute-start(bf16[256,128]{1,0:T(8,128)(2,1)} %get-tuple-element.91), channel_id=1, source_target_pairs={{0,4},{4,8},{8,12},{12,16},{16,20},{20,24},{24,28},{1,5},{5,9},{9,... | collective-permute-start | bytes 196616 | tf_op jit(solution)/shard_map/ppermute | solution.py:15
  135.7 24.5 %collective-permute-start.33 = (bf16[256,128]{1,0:T(8,128)(2,1)}, bf16[256,128]{1,0:T(8,128)(2,1)S(1)}, u32[]{:S(2)}, u32[]{:S(2)}) collective-permute-start(bf16[256,128]{1,0:T(8,128)(2,1)} %get-tuple-element.90), channel_id=1, source_target_pairs={{0,4},{4,8},{8,12},{12,16},{16,20},{20,24},{24,28},{1,5},{5,9},{9,... | collective-permute-start | bytes 196616 | tf_op jit(solution)/shard_map/ppermute | solution.py:15
  147.7 17.1 %collective-permute-start.34 = (bf16[256,128]{1,0:T(8,128)(2,1)S(1)}, bf16[256,128]{1,0:T(8,128)(2,1)S(1)}, u32[]{:S(2)}, u32[]{:S(2)}) collective-permute-start(bf16[256,128]{1,0:T(8,128)(2,1)S(1)} %get-tuple-element.84), channel_id=1, source_target_pairs={{0,4},{4,8},{8,12},{12,16},{16,20},{20,24},{24,28},{1,5},{5,9},{9,... | collective-permute-start | bytes 196616 | tf_op jit(solution)/shard_map/ppermute | solution.py:15
  149.0 25.1 %collective-permute-start.2 = (bf16[256,128]{1,0:T(8,128)(2,1)}, bf16[256,128]{1,0:T(8,128)(2,1)S(1)}, u32[]{:S(2)}, u32[]{:S(2)}) collective-permute-start(bf16[256,128]{1,0:T(8,128)(2,1)} %bitcast.177), channel_id=1, source_target_pairs={{4,0},{8,4},{12,8},{16,12},{20,16},{24,20},{28,24},{5,1},{9,5},{13... | collective-permute-start | bytes 196616 | tf_op jit(solution)/shard_map/ppermute | solution.py:15
  151.1 29.4 %collective-permute-start.3 = (bf16[256,128]{1,0:T(8,128)(2,1)S(1)}, bf16[256,128]{1,0:T(8,128)(2,1)S(1)}, u32[]{:S(2)}, u32[]{:S(2)}) collective-permute-start(bf16[256,128]{1,0:T(8,128)(2,1)S(1)} %bitcast.176), channel_id=1, source_target_pairs={{4,0},{8,4},{12,8},{16,12},{20,16},{24,20},{28,24},{5,1},{9,5},{13... | collective-permute-start | bytes 196616 | tf_op jit(solution)/shard_map/ppermute | solution.py:15
  158.8 33.6 %collective-permute-start.5 = (bf16[256,128]{1,0:T(8,128)(2,1)S(1)}, bf16[256,128]{1,0:T(8,128)(2,1)S(1)}, u32[]{:S(2)}, u32[]{:S(2)}) collective-permute-start(bf16[256,128]{1,0:T(8,128)(2,1)S(1)} %bitcast.173), channel_id=1, source_target_pairs={{1,0},{2,1},{3,2},{5,4},{6,5},{7,6},{9,8},{10,9},{11,10},{13,12},{... | collective-permute-start | bytes 196616 | tf_op jit(solution)/shard_map/ppermute | solution.py:15
  160.2 32.3 %collective-permute-start.6 = (bf16[256,128]{1,0:T(8,128)(2,1)S(1)}, bf16[256,128]{1,0:T(8,128)(2,1)S(1)}, u32[]{:S(2)}, u32[]{:S(2)}) collective-permute-start(bf16[256,128]{1,0:T(8,128)(2,1)S(1)} %bitcast.172), channel_id=1, source_target_pairs={{0,1},{1,2},{2,3},{4,5},{5,6},{6,7},{8,9},{9,10},{10,11},{12,13},{... | collective-permute-start | bytes 196616 | tf_op jit(solution)/shard_map/ppermute | solution.py:15
  170.5 14.3 %collective-permute-start.7 = (bf16[256,128]{1,0:T(8,128)(2,1)S(1)}, bf16[256,128]{1,0:T(8,128)(2,1)S(1)}, u32[]{:S(2)}, u32[]{:S(2)}) collective-permute-start(bf16[256,128]{1,0:T(8,128)(2,1)S(1)} %bitcast.175), channel_id=1, source_target_pairs={{0,4},{4,8},{8,12},{12,16},{16,20},{20,24},{24,28},{1,5},{5,9},{9,... | collective-permute-start | bytes 196616 | tf_op jit(solution)/shard_map/ppermute | solution.py:15
  174.1 12.4 %collective-permute-start.10 = (bf16[256,128]{1,0:T(8,128)(2,1)S(1)}, bf16[256,128]{1,0:T(8,128)(2,1)S(1)}, u32[]{:S(2)}, u32[]{:S(2)}) collective-permute-start(bf16[256,128]{1,0:T(8,128)(2,1)S(1)} %bitcast.174), channel_id=1, source_target_pairs={{0,4},{4,8},{8,12},{12,16},{16,20},{20,24},{24,28},{1,5},{5,9},{9,... | collective-permute-start | bytes 196616 | tf_op jit(solution)/shard_map/ppermute | solution.py:15
  236.3 14.6 %collective-permute-start.12 = (bf16[256,128]{1,0:T(8,128)(2,1)S(1)}, bf16[256,128]{1,0:T(8,128)(2,1)S(1)}, u32[]{:S(2)}, u32[]{:S(2)}) collective-permute-start(bf16[256,128]{1,0:T(8,128)(2,1)S(1)} %bitcast.185), channel_id=1, source_target_pairs={{4,0},{8,4},{12,8},{16,12},{20,16},{24,20},{28,24},{5,1},{9,5},{13... | collective-permute-start | bytes 196616 | tf_op jit(solution)/shard_map/ppermute | solution.py:15
  250.8 15.4 %collective-permute-start.13 = (bf16[256,128]{1,0:T(8,128)(2,1)S(1)}, bf16[256,128]{1,0:T(8,128)(2,1)S(1)}, u32[]{:S(2)}, u32[]{:S(2)}) collective-permute-start(bf16[256,128]{1,0:T(8,128)(2,1)S(1)} %collective-permute-done.12), channel_id=1, source_target_pairs={{1,0},{2,1},{3,2},{5,4},{6,5},{7,6},{9,8},{10,9},{11,10},{13,12},{... | collective-permute-start | bytes 196616 | tf_op jit(solution)/shard_map/ppermute | solution.py:15
  256.6 213.6 %reduce-scatter.5.cloned.1.call-start = ((), (), s32[]{:S(2)}) async-start(), calls=%async_computation.3 | async-start | bytes 1990656 | tf_op jit(solution)/shard_map/reduce_scatter | solution.py:140
  256.7 13.6 %collective-permute-start.14 = (bf16[256,128]{1,0:T(8,128)(2,1)S(1)}, bf16[256,128]{1,0:T(8,128)(2,1)S(1)}, u32[]{:S(2)}, u32[]{:S(2)}) collective-permute-start(bf16[256,128]{1,0:T(8,128)(2,1)S(1)} %bitcast.184), channel_id=1, source_target_pairs={{4,0},{8,4},{12,8},{16,12},{20,16},{24,20},{28,24},{5,1},{9,5},{13... | collective-permute-start | bytes 196616 | tf_op jit(solution)/shard_map/ppermute | solution.py:15
  258.0 16.2 %collective-permute-start.15 = (bf16[256,128]{1,0:T(8,128)(2,1)S(1)}, bf16[256,128]{1,0:T(8,128)(2,1)S(1)}, u32[]{:S(2)}, u32[]{:S(2)}) collective-permute-start(bf16[256,128]{1,0:T(8,128)(2,1)S(1)} %bitcast.183), channel_id=1, source_target_pairs={{4,0},{8,4},{12,8},{16,12},{20,16},{24,20},{28,24},{5,1},{9,5},{13... | collective-permute-start | bytes 196616 | tf_op jit(solution)/shard_map/ppermute | solution.py:15
  259.3 26.7 %collective-permute-start.17 = (bf16[256,128]{1,0:T(8,128)(2,1)S(1)}, bf16[256,128]{1,0:T(8,128)(2,1)S(1)}, u32[]{:S(2)}, u32[]{:S(2)}) collective-permute-start(bf16[256,128]{1,0:T(8,128)(2,1)S(1)} %bitcast.180), channel_id=1, source_target_pairs={{1,0},{2,1},{3,2},{5,4},{6,5},{7,6},{9,8},{10,9},{11,10},{13,12},{... | collective-permute-start | bytes 196616 | tf_op jit(solution)/shard_map/ppermute | solution.py:15
  260.6 25.4 %collective-permute-start.18 = (bf16[256,128]{1,0:T(8,128)(2,1)S(1)}, bf16[256,128]{1,0:T(8,128)(2,1)S(1)}, u32[]{:S(2)}, u32[]{:S(2)}) collective-permute-start(bf16[256,128]{1,0:T(8,128)(2,1)S(1)} %bitcast.179), channel_id=1, source_target_pairs={{0,1},{1,2},{2,3},{4,5},{5,6},{6,7},{8,9},{9,10},{10,11},{12,13},{... | collective-permute-start | bytes 196616 | tf_op jit(solution)/shard_map/ppermute | solution.py:15
  266.2 11.9 %collective-permute-start.19 = (bf16[256,128]{1,0:T(8,128)(2,1)S(1)}, bf16[256,128]{1,0:T(8,128)(2,1)S(1)}, u32[]{:S(2)}, u32[]{:S(2)}) collective-permute-start(bf16[256,128]{1,0:T(8,128)(2,1)S(1)} %bitcast.182), channel_id=1, source_target_pairs={{0,4},{4,8},{8,12},{12,16},{16,20},{20,24},{24,28},{1,5},{5,9},{9,... | collective-permute-start | bytes 196616 | tf_op jit(solution)/shard_map/ppermute | solution.py:15
  270.3 9.8 %collective-permute-start.22 = (bf16[256,128]{1,0:T(8,128)(2,1)S(1)}, bf16[256,128]{1,0:T(8,128)(2,1)S(1)}, u32[]{:S(2)}, u32[]{:S(2)}) collective-permute-start(bf16[256,128]{1,0:T(8,128)(2,1)S(1)} %bitcast.181), channel_id=1, source_target_pairs={{0,4},{4,8},{8,12},{12,16},{16,20},{20,24},{24,28},{1,5},{5,9},{9,... | collective-permute-start | bytes 196616 | tf_op jit(solution)/shard_map/ppermute | solution.py:15
  334.4 175.4 %all-reduce.3.cloned.1.call-start = ((), (), s32[]{:S(2)}) async-start(), calls=%async_computation.4 | async-start | bytes 884736 | tf_op jit(solution)/shard_map/psum | solution.py:142
  428.7 17.2 %collective-permute-start.37 = (bf16[256,128]{1,0:T(8,128)(2,1)S(1)}, bf16[256,128]{1,0:T(8,128)(2,1)S(1)}, u32[]{:S(2)}, u32[]{:S(2)}) collective-permute-start(bf16[256,128]{1,0:T(8,128)(2,1)S(1)} %collective-permute-done.36), channel_id=1, source_target_pairs={{1,0},{2,1},{3,2},{5,4},{6,5},{7,6},{9,8},{10,9},{11,10},{13,12},{... | collective-permute-start | bytes 196616 | tf_op jit(solution)/shard_map/ppermute | solution.py:15
  430.0 19.3 %collective-permute-start.38 = (bf16[256,128]{1,0:T(8,128)(2,1)S(1)}, bf16[256,128]{1,0:T(8,128)(2,1)S(1)}, u32[]{:S(2)}, u32[]{:S(2)}) collective-permute-start(bf16[256,128]{1,0:T(8,128)(2,1)S(1)} %get-tuple-element.82), channel_id=1, source_target_pairs={{4,0},{8,4},{12,8},{16,12},{20,16},{24,20},{28,24},{5,1},{9,5},{13... | collective-permute-start | bytes 196616 | tf_op jit(solution)/shard_map/ppermute | solution.py:15
  431.3 21.9 %collective-permute-start.39 = (bf16[256,128]{1,0:T(8,128)(2,1)S(1)}, bf16[256,128]{1,0:T(8,128)(2,1)S(1)}, u32[]{:S(2)}, u32[]{:S(2)}) collective-permute-start(bf16[256,128]{1,0:T(8,128)(2,1)S(1)} %get-tuple-element.81), channel_id=1, source_target_pairs={{4,0},{8,4},{12,8},{16,12},{20,16},{24,20},{28,24},{5,1},{9,5},{13... | collective-permute-start | bytes 196616 | tf_op jit(solution)/shard_map/ppermute | solution.py:15
  432.6 33.4 %collective-permute-start.41 = (bf16[256,128]{1,0:T(8,128)(2,1)S(1)}, bf16[256,128]{1,0:T(8,128)(2,1)S(1)}, u32[]{:S(2)}, u32[]{:S(2)}) collective-permute-start(bf16[256,128]{1,0:T(8,128)(2,1)S(1)} %get-tuple-element.80), channel_id=1, source_target_pairs={{1,0},{2,1},{3,2},{5,4},{6,5},{7,6},{9,8},{10,9},{11,10},{13,12},{... | collective-permute-start | bytes 196616 | tf_op jit(solution)/shard_map/ppermute | solution.py:15
  433.9 32.2 %collective-permute-start.42 = (bf16[256,128]{1,0:T(8,128)(2,1)S(1)}, bf16[256,128]{1,0:T(8,128)(2,1)S(1)}, u32[]{:S(2)}, u32[]{:S(2)}) collective-permute-start(bf16[256,128]{1,0:T(8,128)(2,1)S(1)} %get-tuple-element.74), channel_id=1, source_target_pairs={{0,1},{1,2},{2,3},{4,5},{5,6},{6,7},{8,9},{9,10},{10,11},{12,13},{... | collective-permute-start | bytes 196616 | tf_op jit(solution)/shard_map/ppermute | solution.py:15
  445.9 12.1 %collective-permute-start.43 = (bf16[256,128]{1,0:T(8,128)(2,1)S(1)}, bf16[256,128]{1,0:T(8,128)(2,1)S(1)}, u32[]{:S(2)}, u32[]{:S(2)}) collective-permute-start(bf16[256,128]{1,0:T(8,128)(2,1)S(1)} %get-tuple-element.73), channel_id=1, source_target_pairs={{0,4},{4,8},{8,12},{12,16},{16,20},{20,24},{24,28},{1,5},{5,9},{9,... | collective-permute-start | bytes 196616 | tf_op jit(solution)/shard_map/ppermute | solution.py:15
  449.3 10.8 %collective-permute-start.46 = (bf16[256,128]{1,0:T(8,128)(2,1)S(1)}, bf16[256,128]{1,0:T(8,128)(2,1)S(1)}, u32[]{:S(2)}, u32[]{:S(2)}) collective-permute-start(bf16[256,128]{1,0:T(8,128)(2,1)S(1)} %get-tuple-element.71), channel_id=1, source_target_pairs={{0,4},{4,8},{8,12},{12,16},{16,20},{20,24},{24,28},{1,5},{5,9},{9,... | collective-permute-start | bytes 196616 | tf_op jit(solution)/shard_map/ppermute | solution.py:15
  (29 other events, 727.8 us)
Sparse Core Ops, SparseCore 0:
  256.7 43.0 reduce-scatter.2
  334.5 41.4 reduce-scatter.4
  470.4 39.3 all-reduce.2
where the time goes:
time: 523 us; the launch traced here: 520 us
  other arithmetic  160 us (31%)
  starting transfers between devices  143 us (27%)
  local copies, waits for them, and re-layouts  119 us (23%)
  waiting for transfers between devices  56.7 us (11%)
  matrix products  25.6 us (5%)
  between operations  15.6 us (3%)
    scatter-add x2, other arithmetic, conv_add_block(): return (totals.at[indices.reshape(-1)].add(terms), None)  149 us
    ppermute x48, starting transfers between devices, shifted(): return lax.ppermute(block, axis, route)  143 us
    gather x4, local copies, waits for them, and re-layouts, one_block(): gathered = extended[indices].reshape(block_span, kernel * channels)  70.1 us
    ppermute x48, waiting for transfers between devices, shifted(): return lax.ppermute(block, axis, route)  28.6 us
    psum x1, waiting for transfers between devices, on_device(): summed_one, summed_two = lax.psum((slab_one, slab_two), 'gy')  28 us
    reshape x2, local copies, waits for them, and re-layouts, conv_add_block(): jnp.dot(pieces, flipped, preferred_element_type=jnp.float32)  15.9 us
    reshape x2, local copies, waits for them, and re-layouts, one_block(): gathered = extended[indices].reshape(block_span, kernel * channels)  15.1 us
    dot_general x2, local copies, waits for them, and re-layouts, weight_add_block(): lax.dot_general(gathered, pieces, (((0,), (0,)), ((), ())), preferred_ele...  11.5 us
  transfers between devices with their start and end apart: 51, of which 14 were waited for; matrix products, arithmetic and copies ran while one was open for 33% of the time, Pallas kernels for 0%

commit v1 on v0

v1 whole, which is shorter than its diff:
```python
import jax
import jax.numpy as jnp
from jax import lax
from jax.experimental import pallas as pl
from jax.experimental.pallas import tpu as pltpu
from jax.sharding import PartitionSpec as P

BLK = 64
UNROLL = 3
F32 = jnp.float32
BF16 = jnp.bfloat16

VM = pl.BlockSpec(memory_space=pltpu.VMEM)
SM = pl.BlockSpec(memory_space=pltpu.SMEM)


def shifted(block, axis, distance):
    devices = range(lax.axis_size(axis))
    route = [(i - distance, i) for i in devices if i - distance in devices]
    return lax.ppermute(block, axis, route)


def deliver(left, middle, right):
    from_left = shifted(left, "gx", -1)
    from_right = shifted(right, "gx", 1)
    down = shifted(jnp.stack((from_left[0], middle[0], from_right[0])), "gy", -1)
    up = shifted(jnp.stack((from_left[2], middle[1], from_right[2])), "gy", 1)
    return from_left[1], from_right[1], down, up


def arrived_at(refs, e):
    left, right, down, up = refs
    return (
        lambda: down[0], lambda: left[...], lambda: up[0], lambda: down[1],
        lambda: up[1], lambda: down[2], lambda: right[...], lambda: up[2],
    )[e]()


def live_mask(count, rows):
    ids = lax.broadcasted_iota(jnp.int32, (rows, 1), 0)
    return ids < count * BLK


def put_outgoing(field_ref, send, out_refs, per):
    left, middle, right = out_refs
    for e in range(8):
        target = left.at[e] if e < 3 else middle.at[e - 3] if e < 5 else right.at[e - 5]
        for s in range(per):
            start = pl.multiple_of(send[e, s] * BLK, BLK)
            target[s * BLK : (s + 1) * BLK, :] = field_ref[pl.ds(start, BLK), :]


def column(table, k):
    lanes = lax.broadcasted_iota(jnp.int32, table.shape, 1)
    return jnp.sum(jnp.where(lanes == k, table, 0.0), axis=1, keepdims=True)


def prepare_kernel(count, send, x_ref, g_ref, masked, upstream, left, middle, right):
    rows = x_ref.shape[0]
    live = live_mask(count[0, 0], rows).astype(F32).astype(BF16)
    masked[...] = x_ref[...] * live
    upstream[...] = g_ref[...] * live
    put_outgoing(masked, send, (left, middle, right), send.shape[1])


def scatter_step(k, g, rule, hi, lo, w, acc):
    rows = g.shape[0]
    pieces = acc.shape[1] // g.shape[1]
    terms = lax.dot_general(g, w[k], (((1,), (1,)), ((), ())), preferred_element_type=F32)
    low = column(lo[...], k)
    wide = jnp.concatenate(
        [jnp.where(low == float(p), terms, 0.0).astype(BF16) for p in range(pieces)], axis=1
    )
    picked = rule[pl.ds(k, 1), :] & (rows - 1) if rows & (rows - 1) == 0 else rule[pl.ds(k, 1), :] % rows
    hot = (lax.broadcasted_iota(jnp.int32, (rows, rows), 0) == picked)
    hot = jnp.where(hot, 1.0, 0.0).astype(BF16)
    return jnp.dot(hot, wide, preferred_element_type=F32)


def scatter_loop(g, rule, hi, lo, w, acc, extra=None):
    acc[...] = jnp.zeros_like(acc)

    @pl.loop(0, w.shape[0] // UNROLL)
    def _(step):
        total = None
        for u in range(UNROLL):
            k = step * UNROLL + u
            part = scatter_step(k, g, rule, hi, lo, w, acc)
            total = part if total is None else total + part
            if extra is not None:
                extra(k)
        acc[...] += total


def split_totals(acc, own, left, middle, right, rows, channels):
    own[...] = acc[:, :channels]
    half = rows // 2
    for j in range(8):
        target = left.at[j] if j < 3 else middle.at[j - 3] if j < 5 else right.at[j - 5]
        base = (j % 2) * half
        col = (1 + j // 2) * channels
        target[...] = acc[base : base + half, col : col + channels].astype(BF16)


def first_scatter_kernel(g, rule, hi, lo, w, own, left, middle, right, acc):
    rows, channels = g.shape
    scatter_loop(g[...], rule, hi, lo, w, acc)
    split_totals(acc, own, left, middle, right, rows, channels)


def fill_table(field, refs, table):
    rows, channels = field.shape
    half = rows // 2
    table[:, :channels] = field[...]
    for j in range(8):
        base = (j % 2) * half
        col = (1 + j // 2) * channels
        table[base : base + half, col : col + channels] = arrived_at(refs, 7 - j)


def gather_step(k, hi, lo, table, channels):
    rows = table.shape[0]
    high = column(hi[...], k)
    low = column(lo[...], k)
    ids = lax.broadcasted_iota(jnp.int32, (rows, rows), 1).astype(F32)
    hot = jnp.where(ids == high, 1.0, 0.0).astype(BF16)
    found = jnp.dot(hot, table[...], preferred_element_type=F32)
    picked = jnp.zeros((rows, channels), F32)
    for p in range(table.shape[1] // channels):
        picked = jnp.where(low == float(p), found[:, p * channels : (p + 1) * channels], picked)
    return picked.astype(BF16)


def first_gather_kernel(
    count, send, field, a, b, c, d, hi, lo, w, pre, gathered, hidden, left, middle, right, table
):
    rows, channels = field.shape
    fill_table(field, (a, b, c, d), table)
    pre[...] = jnp.zeros_like(pre)

    @pl.loop(0, w.shape[0] // UNROLL)
    def _(step):
        total = None
        for u in range(UNROLL):
            k = step * UNROLL + u
            picked = gather_step(k, hi, lo, table, channels)
            gathered[k] = picked
            part = jnp.dot(picked, w[k], preferred_element_type=F32)
            total = part if total is None else total + part
        pre[...] += total

    live = live_mask(count[0, 0], rows).astype(F32)
    v = pre[...] * live
    pre[...] = v
    hidden[...] = (v / (1.0 + jnp.exp(-v))).astype(BF16)
    put_outgoing(hidden, send, (left, middle, right), send.shape[1])


def add_returned(send, own, refs, total, per):
    total[...] = own[...]
    for e in range(8):
        block = arrived_at(refs, e).astype(F32)
        for s in range(per):
            start = pl.multiple_of(send[7 - e, s] * BLK, BLK)
            total[pl.ds(start, BLK), :] += block[s * BLK : (s + 1) * BLK, :]


def second_scatter_kernel(
    count, send, grad_own, a, b, c, d, pre, gathered, rule, hi, lo, w,
    own, left, middle, right, partial, acc, total, grad
):
    rows, channels = pre.shape
    add_returned(send, grad_own, (a, b, c, d), total, send.shape[1])
    live = live_mask(count[0, 0], rows).astype(F32)
    v = pre[...]
    s = 1.0 / (1.0 + jnp.exp(-v))
    grad[...] = (total[...] * s * (1.0 + v * (1.0 - s)) * live).astype(BF16)
    g = grad[...]

    def extra(k):
        partial[k] = lax.dot_general(
            gathered[k], g, (((0,), (0,)), ((), ())), preferred_element_type=F32
        )

    scatter_loop(g, rule, hi, lo, w, acc, extra)
    split_totals(acc, own, left, middle, right, rows, channels)


def second_gather_kernel(count, field, a, b, c, d, hi, lo, w, g, out, partial, table, total):
    rows, channels = field.shape
    fill_table(field, (a, b, c, d), table)
    total[...] = jnp.zeros_like(total)
    upstream = g[...]

    @pl.loop(0, w.shape[0] // UNROLL)
    def _(step):
        summed = None
        for u in range(UNROLL):
            k = step * UNROLL + u
            picked = gather_step(k, hi, lo, table, channels)
            partial[k] = lax.dot_general(
                picked, upstream, (((0,), (0,)), ((), ())), preferred_element_type=F32
            )
            part = jnp.dot(picked, w[k], preferred_element_type=F32)
            summed = part if summed is None else summed + part
        total[...] += summed

    live = live_mask(count[0, 0], rows).astype(F32)
    out[...] = (total[...] * live).astype(BF16)


def finish_kernel(count, send, own, a, b, c, d, out, total):
    rows = own.shape[0]
    add_returned(send, own, (a, b, c, d), total, send.shape[1])
    out[...] = (total[...] * live_mask(count[0, 0], rows).astype(F32)).astype(BF16)


def call(kernel, out_shape, in_specs, scratch, flops=0, moved=0):
    return pl.pallas_call(
        kernel,
        out_shape=out_shape,
        in_specs=in_specs,
        out_specs=tuple([VM] * len(out_shape)),
        scratch_shapes=scratch,
        compiler_params=pltpu.CompilerParams(vmem_limit_bytes=48 << 20),
        cost_estimate=pl.CostEstimate(flops=flops, bytes_accessed=moved, transcendentals=0),
    )


def on_device(features, cotangent, weight_one, weight_two, block_count, send_list, rulebook):
    field, cot = features[0, 0], cotangent[0, 0]
    send, rule = send_list[0, 0], rulebook[0, 0]
    rows, channels = field.shape
    kernel = rule.shape[0]
    slot = send.shape[1] * BLK
    shape = jax.ShapeDtypeStruct
    wide = (rows, channels * (1 + 8 * slot // rows))
    columns = jnp.pad(rule.T, ((0, 0), (0, 128 - kernel)))
    hi = (columns % rows).astype(F32)
    lo = (columns // rows).astype(F32)
    flops = 2 * kernel * rows * rows * wide[1]
    moved = 8 << 20
    rows_bf = shape((rows, channels), BF16)
    rows_f = shape((rows, channels), F32)
    groups = (
        shape((3, slot, channels), BF16), shape((2, slot, channels), BF16),
        shape((3, slot, channels), BF16),
    )
    grads = shape((kernel, channels, channels), F32)
    table = pltpu.VMEM(wide, BF16)
    acc = pltpu.VMEM(wide, F32)
    plain = pltpu.VMEM((rows, channels), F32)

    masked, upstream, *out_masked = call(
        prepare_kernel, (rows_bf, rows_bf) + groups, [SM, SM, VM, VM], []
    )(block_count, send, field, cot)
    halo_one = deliver(*out_masked)
    own_two, *back_two = call(
        first_scatter_kernel, (rows_f,) + groups, [VM] * 5, [acc], flops, moved
    )(upstream, rule, hi, lo, weight_two)
    arrived_two = deliver(*back_two)
    pre, gathered, hidden, *out_hidden = call(
        first_gather_kernel,
        (rows_f, shape((kernel, rows, channels), BF16), rows_bf) + groups,
        [SM, SM] + [VM] * 8, [table], flops, moved,
    )(block_count, send, masked, *halo_one, hi, lo, weight_one)
    halo_two = deliver(*out_hidden)
    own_one, *rest = call(
        second_scatter_kernel, (rows_f,) + groups + (grads,),
        [SM, SM] + [VM] * 11,
        [acc, plain, pltpu.VMEM((rows, channels), BF16)], flops, moved,
    )(block_count, send, own_two, *arrived_two, pre, gathered, rule, hi, lo, weight_one)
    *back_one, partial_one = rest
    arrived_one = deliver(*back_one)
    output, partial_two = call(
        second_gather_kernel, (rows_bf, grads), [SM] + [VM] * 9, [table, plain], flops, moved
    )(block_count, hidden, *halo_two, hi, lo, weight_two, upstream)
    (grad_input,) = call(finish_kernel, (rows_bf,), [SM, SM] + [VM] * 5, [plain])(
        block_count, send, own_one, *arrived_one
    )
    device_total = lax.axis_size("gx") * lax.axis_size("gy")
    slab_one = lax.psum_scatter(partial_one, "gx", scatter_dimension=1, tiled=True)
    slab_two = lax.psum_scatter(partial_two, "gx", scatter_dimension=1, tiled=True)
    summed_one, summed_two = lax.psum((slab_one, slab_two), "gy")
    return (
        output[None, None],
        grad_input[None, None],
        summed_one / device_total,
        summed_two / device_total,
    )


def solution(mesh):
    placed = (
        P("gx", "gy", None, None),
        P("gx", "gy", None, None),
        P(),
        P(),
        P("gx", "gy"),
        P("gx", "gy", None, None),
        P("gx", "gy", None, None),
    )
    return jax.shard_map(
        on_device,
        mesh=mesh,
        in_specs=placed,
        out_specs=(
            P("gx", "gy", None, None),
            P("gx", "gy", None, None),
            P(None, "gx", None),
            P(None, "gx", None),
        ),
        check_vma=False,
    )
```

time: 523 us -> 228 us (0.44)
  other arithmetic: 160 us -> 2.29 us
  local copies, waits for them, and re-layouts: 119 us -> 5.67 us
  starting transfers between devices: 143 us -> 42.3 us
  Pallas kernels: 0 us -> 79.4 us
  waiting for transfers between devices: 56.7 us -> 83.3 us
  matrix products: 25.6 us -> 0 us
    scatter-add x4 -> x0, other arithmetic: 153 us -> none  [the longest x2 149 us: conv_add_block(): return (totals.at[indices.reshape(-1)].add(terms), None)]
    ppermute x48 -> x16, starting transfers between devices: 143 us -> 42.2 us  [shifted(): return lax.ppermute(block, axis, route)]
    pallas_call x0 -> x6, Pallas kernels: none -> 79.4 us  [the longest x1 23 us: on_device(): call(second_gather_kernel, (rows_bf, grads), [SM] + [VM] * 9, [table, pla...]
    gather x6 -> x0, local copies, waits for them, and re-layouts: 71.4 us -> none  [the longest x4 70.1 us: one_block(): gathered = extended[indices].reshape(block_span, kernel * channels)]
    reduce_scatter x1, waiting for transfers between devices: 0.02 us -> 39.8 us  [on_device(): lax.psum_scatter(partial_two, 'gx', scatter_dimension=1, tiled=True)]
    reshape x6 -> x0, local copies, waits for them, and re-layouts: 31.3 us -> none  [the longest x2 15.9 us: conv_add_block(): jnp.dot(pieces, flipped, preferred_element_type=jnp.float32)]
    dot_general x6 -> x0, matrix products: 25.6 us -> none  [the longest x2 9.36 us: conv_add_block(): jnp.dot(pieces, flipped, preferred_element_type=jnp.float32)]
    dot_general x2 -> x0, local copies, waits for them, and re-layouts: 11.5 us -> none  [weight_add_block(): lax.dot_general(gathered, pieces, (((0,), (0,)), ((), ())), preferred_ele...]
  transfers between devices with their start and end apart: 51 -> 19, of which waited for: 14 -> 8; matrix products, arithmetic and copies ran while one was open for 33% -> 1% of each run, Pallas kernels for 0% -> 25%
where the time goes in v1:
time: 228 us
  waiting for transfers between devices  83.3 us (37%)
  Pallas kernels  79.4 us (35%)
  starting transfers between devices  42.3 us (19%)
  between operations  14.8 us (6%)
  local copies, waits for them, and re-layouts  5.67 us (2%)
  other arithmetic  2.29 us (1%)
    ppermute x16, starting transfers between devices, shifted(): return lax.ppermute(block, axis, route)  42.2 us
    reduce_scatter x1, waiting for transfers between devices, on_device(): lax.psum_scatter(partial_two, 'gx', scatter_dimension=1, tiled=True)  39.8 us
    psum x1, waiting for transfers between devices, on_device(): summed_one, summed_two = lax.psum((slab_one, slab_two), 'gy')  25.1 us
    pallas_call x1, Pallas kernels, on_device(): call(second_gather_kernel, (rows_bf, grads), [SM] + [VM] * 9, [table, pla...  23 us
    pallas_call x1, Pallas kernels, on_device(): call(second_scatter_kernel, (rows_f,) + groups + (grads,), [SM, SM] + [VM...  20.7 us
    ppermute x16, waiting for transfers between devices, shifted(): return lax.ppermute(block, axis, route)  18.3 us
    pallas_call x1, Pallas kernels, on_device(): call(first_gather_kernel, (rows_f, shape((kernel, rows, channels), BF16),...  17.4 us
    pallas_call x1, Pallas kernels, on_device(): call(first_scatter_kernel, (rows_f,) + groups, [VM] * 5, [acc], flops, mo...  16.1 us
  transfers between devices with their start and end apart: 19, of which 8 were waited for; matrix products, arithmetic and copies ran while one was open for 1% of the time, Pallas kernels for 25%

profile of v1, /device:TPU:0, one launch (start us, length us, event | category | flops | bytes accessed | tf_op | source)
XLA Modules:
  0.0 227.7 jit_solution(6238798587398875277)
XLA Ops:
  11.2 1.3 collective-permute-start
  12.5 3.0 %collective-permute-start.1 = (bf16[3,256,128]{2,1,0:T(8,128)(2,1)S(1)}, bf16[3,256,128]{2,1,0:T(8,128)(2,1)S(1)}, u32[]{:S(2)}, u32[]{:S(2)}) collective-permute-start(bf16[3,256,128]{2,1,0:T(8,128)(2,1)S(1)} %get-tuple-element.28), channel_id=1, source_target_pairs={{0,4},{4,8},{8,12},{12,16},{16,20},{20,24},{24,28},{1,5},{5,9},{9,... | collective-permute-start | bytes 589832 | tf_op jit(solution)/shard_map/ppermute | solution.py:20
  15.5 1.0 copy.12
  17.6 1.2 copy-done.3
  18.7 16.1 %shard_map.105 = (f32[512,128]{1,0:T(8,128)S(1)}, bf16[3,256,128]{2,1,0:T(8,128)(2,1)S(1)}, bf16[2,256,128]{2,1,0:T(8,128)(2,1)S(1)}, bf16[3,256,128]{2,1,0:T(8,128)(2,1)S(1)}) custom-call(bf16[512,128]{1,0:T(8,128)(2,1)S(1)} %get-tuple-element.34.g, s32[27,512]{1,0:T(8,128)S(1)} %bitcast.29, f32[512,128]{1,0:T(8,128)S(1)} %get-tuple-element.51.hi, ...), custom_call_target="tpu_custom_call" | custom-call | flops 9059696640 | bytes 8388608 | tf_op jit(solution)/shard_map/pallas_call | solution.py:258
  34.9 1.3 collective-permute-start.8
  36.2 5.1 %collective-permute-start.9 = (bf16[3,256,128]{2,1,0:T(8,128)(2,1)S(1)}, bf16[3,256,128]{2,1,0:T(8,128)(2,1)S(1)}, u32[]{:S(2)}, u32[]{:S(2)}) collective-permute-start(bf16[3,256,128]{2,1,0:T(8,128)(2,1)S(1)} %get-tuple-element.38), channel_id=1, source_target_pairs={{0,4},{4,8},{8,12},{12,16},{16,20},{20,24},{24,28},{1,5},{5,9},{9,... | collective-permute-start | bytes 589832 | tf_op jit(solution)/shard_map/ppermute | solution.py:20
  41.4 3.6 %collective-permute-start.3 = (bf16[3,256,128]{2,1,0:T(8,128)(2,1)S(1)}, bf16[3,256,128]{2,1,0:T(8,128)(2,1)S(1)}, u32[]{:S(2)}, u32[]{:S(2)}) collective-permute-start(bf16[3,256,128]{2,1,0:T(8,128)(2,1)S(1)} %pad_maximum_fusion.1), channel_id=1, source_target_pairs={{0,1},{1,2},{2,3},{4,5},{5,6},{6,7},{8,9},{9,10},{10,11},{12,13},{... | collective-permute-start | bytes 589832 | tf_op jit(solution)/shard_map/ppermute | solution.py:20
  45.1 1.3 collective-permute-start.2
  46.5 1.3 collective-permute-start.10
  47.8 5.2 %collective-permute-start.11 = (bf16[3,256,128]{2,1,0:T(8,128)(2,1)S(1)}, bf16[3,256,128]{2,1,0:T(8,128)(2,1)S(1)}, u32[]{:S(2)}, u32[]{:S(2)}) collective-permute-start(bf16[3,256,128]{2,1,0:T(8,128)(2,1)S(1)} %pad_maximum_fusion.5), channel_id=1, source_target_pairs={{0,1},{1,2},{2,3},{4,5},{5,6},{6,7},{8,9},{9,10},{10,11},{12,13},{... | collective-permute-start | bytes 589832 | tf_op jit(solution)/shard_map/ppermute | solution.py:20
  53.1 1.3 collective-permute-done.2.c
  54.4 17.4 %shard_map.103 = (f32[512,128]{1,0:T(8,128)S(1)}, bf16[27,512,128]{2,1,0:T(8,128)(2,1)}, bf16[512,128]{1,0:T(8,128)(2,1)S(1)}, bf16[3,256,128]{2,1,0:T(8,128)(2,...) custom-call(s32[1,1]{1,0:T(1,128)S(6)} %copy.23.count, s32[8,4]{1,0:T(8,128)S(1)} %copy.13.send, ...), custom_call_target="tpu_custom_call" | custom-call | flops 9059696640 | bytes 8388608 | tf_op jit(solution)/shard_map/pallas_call | solution.py:262
  71.7 20.7 %shard_map.106 = (f32[512,128]{1,0:T(8,128)S(1)}, bf16[3,256,128]{2,1,0:T(8,128)(2,1)S(1)}, bf16[2,256,128]{2,1,0:T(8,128)(2,1)S(1)}, bf16[3,256,128]{2,1,0:T(8,128)(2,1)S(1)}, f32[27,128,128]{2,1,0:T(8,128)}) custom-call(s32[1,1]{1,0:T(1,128)S(6)} %copy.23.count, s32[8,4]{1,0:T(8,128)S(1)} %copy.13.send, f32[512,128]{1,0:T(8,128)S(1)} %get-tuple-element.36.grad_own, ...), custom_call_target="tpu_custom_call" | custom-call | flops 9059696640 | bytes 8388608 | tf_op jit(solution)/shard_map/pallas_call | solution.py:268
  92.5 1.4 collective-permute-start.4
  94.0 3.5 %collective-permute-start.5 = (bf16[3,256,128]{2,1,0:T(8,128)(2,1)S(1)}, bf16[3,256,128]{2,1,0:T(8,128)(2,1)S(1)}, u32[]{:S(2)}, u32[]{:S(2)}) collective-permute-start(bf16[3,256,128]{2,1,0:T(8,128)(2,1)S(1)} %get-tuple-element.32), channel_id=1, source_target_pairs={{0,4},{4,8},{8,12},{12,16},{16,20},{20,24},{24,28},{1,5},{5,9},{9,... | collective-permute-start | bytes 589832 | tf_op jit(solution)/shard_map/ppermute | solution.py:20
  97.5 1.0 collective-permute-done.5
  98.5 3.5 %collective-permute-start.7 = (bf16[3,256,128]{2,1,0:T(8,128)(2,1)S(1)}, bf16[3,256,128]{2,1,0:T(8,128)(2,1)S(1)}, u32[]{:S(2)}, u32[]{:S(2)}) collective-permute-start(bf16[3,256,128]{2,1,0:T(8,128)(2,1)S(1)} %pad_maximum_fusion.3), channel_id=1, source_target_pairs={{0,1},{1,2},{2,3},{4,5},{5,6},{6,7},{8,9},{9,10},{10,11},{12,13},{... | collective-permute-start | bytes 589832 | tf_op jit(solution)/shard_map/ppermute | solution.py:20
  102.0 1.3 collective-permute-start.6
  103.3 1.8 collective-permute-done.7.d
  105.1 4.4 %collective-permute-done.6.c = bf16[3,256,128]{2,1,0:T(8,128)(2,1)S(1)} collective-permute-done((bf16[3,256,128]{2,1,0:T(8,128)(2,1)S(1)}, bf16[3,256,128]{2,1,0:T(8,128)(2,1)S(1)}, u32[]{:S(2)}, u32[]{:S(2)}) %collective-permute-start.6) | collective-permute-done | bytes 196640 | tf_op jit(solution)/shard_map/ppermute | solution.py:20
  109.6 23.0 %shard_map.104 = (bf16[512,128]{1,0:T(8,128)(2,1)}, f32[27,128,128]{2,1,0:T(8,128)}) custom-call(s32[1,1]{1,0:T(1,128)S(6)} %copy.23.count, bf16[512,128]{1,0:T(8,128)(2,1)S(1)} %get-tuple-element.30.field, bf16[256,128]{1,0:T(8,128)(2,1)S(1)} %get-tuple-element.66.a, bf16[256,128]{1,0:T(8,128)(2,1)S(1)} %get-tuple-element.69.b, ...), custom_call_target="tpu_custom_call" | custom-call | flops 9059696640 | bytes 8388608 | tf_op jit(solution)/shard_map/pallas_call | solution.py:275
  132.7 1.3 collective-permute-start.12
  134.0 4.5 %collective-permute-start.13 = (bf16[3,256,128]{2,1,0:T(8,128)(2,1)S(1)}, bf16[3,256,128]{2,1,0:T(8,128)(2,1)S(1)}, u32[]{:S(2)}, u32[]{:S(2)}) collective-permute-start(bf16[3,256,128]{2,1,0:T(8,128)(2,1)S(1)} %get-tuple-element.44), channel_id=1, source_target_pairs={{0,4},{4,8},{8,12},{12,16},{16,20},{20,24},{24,28},{1,5},{5,9},{9,... | collective-permute-start | bytes 589832 | tf_op jit(solution)/shard_map/ppermute | solution.py:20
  138.5 39.8 %reduce-scatter.5.cloned.1.call-done = f32[27,16,128]{2,1,0:T(8,128)} async-done(((f32[27,128,128]{2,1,0:T(8,128)}), f32[27,16,128]{2,1,0:T(8,128)}) %reduce-scatter.5.cloned.1.call-update) | async-done | bytes 221200 | tf_op jit(solution)/shard_map/reduce_scatter | solution.py:283
  178.4 3.4 %collective-permute-start.15 = (bf16[3,256,128]{2,1,0:T(8,128)(2,1)S(1)}, bf16[3,256,128]{2,1,0:T(8,128)(2,1)S(1)}, u32[]{:S(2)}, u32[]{:S(2)}) collective-permute-start(bf16[3,256,128]{2,1,0:T(8,128)(2,1)S(1)} %pad_maximum_fusion.7), channel_id=1, source_target_pairs={{0,1},{1,2},{2,3},{4,5},{5,6},{6,7},{8,9},{9,10},{10,11},{12,13},{... | collective-permute-start | bytes 589832 | tf_op jit(solution)/shard_map/ppermute | solution.py:20
  181.9 1.3 collective-permute-start.14
  183.2 2.8 %collective-permute-done.15.d = bf16[3,256,128]{2,1,0:T(8,128)(2,1)S(1)} collective-permute-done((bf16[3,256,128]{2,1,0:T(8,128)(2,1)S(1)}, bf16[3,256,128]{2,1,0:T(8,128)(2,1)S(1)}, u32[]{:S(2)}, u32[]{:S(2)}) %collective-permute-start.15) | collective-permute-done | bytes 196640 | tf_op jit(solution)/shard_map/ppermute | solution.py:20
  186.0 6.9 %collective-permute-done.14.c = bf16[3,256,128]{2,1,0:T(8,128)(2,1)S(1)} collective-permute-done((bf16[3,256,128]{2,1,0:T(8,128)(2,1)S(1)}, bf16[3,256,128]{2,1,0:T(8,128)(2,1)S(1)}, u32[]{:S(2)}, u32[]{:S(2)}) %collective-permute-start.14) | collective-permute-done | bytes 196640 | tf_op jit(solution)/shard_map/ppermute | solution.py:20
  192.8 1.5 shard_map.107
  194.3 25.1 %all-reduce.4.cloned.1.call-done = (f32[27,16,128]{2,1,0:T(8,128)}, f32[27,16,128]{2,1,0:T(8,128)}) async-done(((f32[27,16,128]{2,1,0:T(8,128)}, f32[27,16,128]{2,1,0:T(8,128)}), (f32[27,16,128]{2,1,0:T(8,128)}, f32[27,16,128]{2,1,0:T(8,128)})) %all-reduce.4.cloned.1.call-update) | async-done | bytes 442384 | tf_op jit(solution)/shard_map/psum | solution.py:284
  219.4 1.8 broadcast_multiply_fusion
  (50 shorter events, 5.0 us)
Async XLA Ops:
  7.2 131.3 %reduce-scatter.3.cloned.1.call-start = ((), (), s32[]{:S(2)}) async-start(), calls=%async_computation.2 | async-start | bytes 1990656 | tf_op jit(solution)/shard_map/reduce_scatter | solution.py:282
  8.6 0.9 copy-start
  9.5 0.9 copy-start.1
  11.2 30.2 %collective-permute-start = (bf16[3,256,128]{2,1,0:T(8,128)(2,1)S(1)}, bf16[3,256,128]{2,1,0:T(8,128)(2,1)S(1)}, u32[]{:S(2)}, u32[]{:S(2)}) collective-permute-start(bf16[3,256,128]{2,1,0:T(8,128)(2,1)S(1)} %get-tuple-element.27), channel_id=1, source_target_pairs={{4,0},{8,4},{12,8},{16,12},{20,16},{24,20},{28,24},{5,1},{9,5},{13... | collective-permute-start | bytes 589832 | tf_op jit(solution)/shard_map/ppermute | solution.py:20
  12.5 28.9 %collective-permute-start.1 = (bf16[3,256,128]{2,1,0:T(8,128)(2,1)S(1)}, bf16[3,256,128]{2,1,0:T(8,128)(2,1)S(1)}, u32[]{:S(2)}, u32[]{:S(2)}) collective-permute-start(bf16[3,256,128]{2,1,0:T(8,128)(2,1)S(1)} %get-tuple-element.28), channel_id=1, source_target_pairs={{0,4},{4,8},{8,12},{12,16},{16,20},{20,24},{24,28},{1,5},{5,9},{9,... | collective-permute-start | bytes 589832 | tf_op jit(solution)/shard_map/ppermute | solution.py:20
  17.6 1.2 copy-start.3
  34.9 11.5 %collective-permute-start.8 = (bf16[3,256,128]{2,1,0:T(8,128)(2,1)S(1)}, bf16[3,256,128]{2,1,0:T(8,128)(2,1)S(1)}, u32[]{:S(2)}, u32[]{:S(2)}) collective-permute-start(bf16[3,256,128]{2,1,0:T(8,128)(2,1)S(1)} %get-tuple-element.37), channel_id=1, source_target_pairs={{4,0},{8,4},{12,8},{16,12},{20,16},{24,20},{28,24},{5,1},{9,5},{13... | collective-permute-start | bytes 589832 | tf_op jit(solution)/shard_map/ppermute | solution.py:20
  36.2 10.3 %collective-permute-start.9 = (bf16[3,256,128]{2,1,0:T(8,128)(2,1)S(1)}, bf16[3,256,128]{2,1,0:T(8,128)(2,1)S(1)}, u32[]{:S(2)}, u32[]{:S(2)}) collective-permute-start(bf16[3,256,128]{2,1,0:T(8,128)(2,1)S(1)} %get-tuple-element.38), channel_id=1, source_target_pairs={{0,4},{4,8},{8,12},{12,16},{16,20},{20,24},{24,28},{1,5},{5,9},{9,... | collective-permute-start | bytes 589832 | tf_op jit(solution)/shard_map/ppermute | solution.py:20
  41.3 13.1 %copy-start.2 = (bf16[27,128,128]{2,1,0:T(8,128)(2,1)S(1)}, bf16[27,128,128]{2,1,0:T(8,128)(2,1)}, u32[]{:S(2)}) copy-start(bf16[27,128,128]{2,1,0:T(8,128)(2,1)} %w.7) | copy-start | bytes 2654212
  41.4 11.6 %collective-permute-start.3 = (bf16[3,256,128]{2,1,0:T(8,128)(2,1)S(1)}, bf16[3,256,128]{2,1,0:T(8,128)(2,1)S(1)}, u32[]{:S(2)}, u32[]{:S(2)}) collective-permute-start(bf16[3,256,128]{2,1,0:T(8,128)(2,1)S(1)} %pad_maximum_fusion.1), channel_id=1, source_target_pairs={{0,1},{1,2},{2,3},{4,5},{5,6},{6,7},{8,9},{9,10},{10,11},{12,13},{... | collective-permute-start | bytes 589832 | tf_op jit(solution)/shard_map/ppermute | solution.py:20
  45.1 9.3 %collective-permute-start.2 = (bf16[3,256,128]{2,1,0:T(8,128)(2,1)S(1)}, bf16[3,256,128]{2,1,0:T(8,128)(2,1)S(1)}, u32[]{:S(2)}, u32[]{:S(2)}) collective-permute-start(bf16[3,256,128]{2,1,0:T(8,128)(2,1)S(1)} %pad_maximum_fusion), channel_id=1, source_target_pairs={{1,0},{2,1},{3,2},{5,4},{6,5},{7,6},{9,8},{10,9},{11,10},{13,12},{... | collective-permute-start | bytes 589832 | tf_op jit(solution)/shard_map/ppermute | solution.py:20
  46.5 25.2 %collective-permute-start.10 = (bf16[3,256,128]{2,1,0:T(8,128)(2,1)S(1)}, bf16[3,256,128]{2,1,0:T(8,128)(2,1)S(1)}, u32[]{:S(2)}, u32[]{:S(2)}) collective-permute-start(bf16[3,256,128]{2,1,0:T(8,128)(2,1)S(1)} %pad_maximum_fusion.4), channel_id=1, source_target_pairs={{1,0},{2,1},{3,2},{5,4},{6,5},{7,6},{9,8},{10,9},{11,10},{13,12},{... | collective-permute-start | bytes 589832 | tf_op jit(solution)/shard_map/ppermute | solution.py:20
  47.8 23.9 %collective-permute-start.11 = (bf16[3,256,128]{2,1,0:T(8,128)(2,1)S(1)}, bf16[3,256,128]{2,1,0:T(8,128)(2,1)S(1)}, u32[]{:S(2)}, u32[]{:S(2)}) collective-permute-start(bf16[3,256,128]{2,1,0:T(8,128)(2,1)S(1)} %pad_maximum_fusion.5), channel_id=1, source_target_pairs={{0,1},{1,2},{2,3},{4,5},{5,6},{6,7},{8,9},{9,10},{10,11},{12,13},{... | collective-permute-start | bytes 589832 | tf_op jit(solution)/shard_map/ppermute | solution.py:20
  92.4 17.1 %copy-start.4 = (bf16[27,128,128]{2,1,0:T(8,128)(2,1)S(1)}, bf16[27,128,128]{2,1,0:T(8,128)(2,1)}, u32[]{:S(2)}) copy-start(bf16[27,128,128]{2,1,0:T(8,128)(2,1)} %w.6) | copy-start | bytes 2654212
  92.5 85.9 %reduce-scatter.5.cloned.1.call-start = ((), (), s32[]{:S(2)}) async-start(), calls=%async_computation.3 | async-start | bytes 1990656 | tf_op jit(solution)/shard_map/reduce_scatter | solution.py:283
  92.5 4.9 %collective-permute-start.4 = (bf16[3,256,128]{2,1,0:T(8,128)(2,1)S(1)}, bf16[3,256,128]{2,1,0:T(8,128)(2,1)S(1)}, u32[]{:S(2)}, u32[]{:S(2)}) collective-permute-start(bf16[3,256,128]{2,1,0:T(8,128)(2,1)S(1)} %get-tuple-element.31), channel_id=1, source_target_pairs={{4,0},{8,4},{12,8},{16,12},{20,16},{24,20},{28,24},{5,1},{9,5},{13... | collective-permute-start | bytes 589832 | tf_op jit(solution)/shard_map/ppermute | solution.py:20
  94.0 4.5 %collective-permute-start.5 = (bf16[3,256,128]{2,1,0:T(8,128)(2,1)S(1)}, bf16[3,256,128]{2,1,0:T(8,128)(2,1)S(1)}, u32[]{:S(2)}, u32[]{:S(2)}) collective-permute-start(bf16[3,256,128]{2,1,0:T(8,128)(2,1)S(1)} %get-tuple-element.32), channel_id=1, source_target_pairs={{0,4},{4,8},{8,12},{12,16},{16,20},{20,24},{24,28},{1,5},{5,9},{9,... | collective-permute-start | bytes 589832 | tf_op jit(solution)/shard_map/ppermute | solution.py:20
  98.5 6.6 %collective-permute-start.7 = (bf16[3,256,128]{2,1,0:T(8,128)(2,1)S(1)}, bf16[3,256,128]{2,1,0:T(8,128)(2,1)S(1)}, u32[]{:S(2)}, u32[]{:S(2)}) collective-permute-start(bf16[3,256,128]{2,1,0:T(8,128)(2,1)S(1)} %pad_maximum_fusion.3), channel_id=1, source_target_pairs={{0,1},{1,2},{2,3},{4,5},{5,6},{6,7},{8,9},{9,10},{10,11},{12,13},{... | collective-permute-start | bytes 589832 | tf_op jit(solution)/shard_map/ppermute | solution.py:20
  102.0 7.6 %collective-permute-start.6 = (bf16[3,256,128]{2,1,0:T(8,128)(2,1)S(1)}, bf16[3,256,128]{2,1,0:T(8,128)(2,1)S(1)}, u32[]{:S(2)}, u32[]{:S(2)}) collective-permute-start(bf16[3,256,128]{2,1,0:T(8,128)(2,1)S(1)} %pad_maximum_fusion.2), channel_id=1, source_target_pairs={{1,0},{2,1},{3,2},{5,4},{6,5},{7,6},{9,8},{10,9},{11,10},{13,12},{... | collective-permute-start | bytes 589832 | tf_op jit(solution)/shard_map/ppermute | solution.py:20
  132.6 86.8 %all-reduce.4.cloned.1.call-start = ((), (), s32[]{:S(2)}) async-start(), calls=%async_computation.4 | async-start | bytes 884736 | tf_op jit(solution)/shard_map/psum | solution.py:284
  132.7 5.8 %collective-permute-start.12 = (bf16[3,256,128]{2,1,0:T(8,128)(2,1)S(1)}, bf16[3,256,128]{2,1,0:T(8,128)(2,1)S(1)}, u32[]{:S(2)}, u32[]{:S(2)}) collective-permute-start(bf16[3,256,128]{2,1,0:T(8,128)(2,1)S(1)} %get-tuple-element.43), channel_id=1, source_target_pairs={{4,0},{8,4},{12,8},{16,12},{20,16},{24,20},{28,24},{5,1},{9,5},{13... | collective-permute-start | bytes 589832 | tf_op jit(solution)/shard_map/ppermute | solution.py:20
  134.0 44.4 %collective-permute-start.13 = (bf16[3,256,128]{2,1,0:T(8,128)(2,1)S(1)}, bf16[3,256,128]{2,1,0:T(8,128)(2,1)S(1)}, u32[]{:S(2)}, u32[]{:S(2)}) collective-permute-start(bf16[3,256,128]{2,1,0:T(8,128)(2,1)S(1)} %get-tuple-element.44), channel_id=1, source_target_pairs={{0,4},{4,8},{8,12},{12,16},{16,20},{20,24},{24,28},{1,5},{5,9},{9,... | collective-permute-start | bytes 589832 | tf_op jit(solution)/shard_map/ppermute | solution.py:20
  178.4 7.5 %collective-permute-start.15 = (bf16[3,256,128]{2,1,0:T(8,128)(2,1)S(1)}, bf16[3,256,128]{2,1,0:T(8,128)(2,1)S(1)}, u32[]{:S(2)}, u32[]{:S(2)}) collective-permute-start(bf16[3,256,128]{2,1,0:T(8,128)(2,1)S(1)} %pad_maximum_fusion.7), channel_id=1, source_target_pairs={{0,1},{1,2},{2,3},{4,5},{5,6},{6,7},{8,9},{9,10},{10,11},{12,13},{... | collective-permute-start | bytes 589832 | tf_op jit(solution)/shard_map/ppermute | solution.py:20
  181.9 10.9 %collective-permute-start.14 = (bf16[3,256,128]{2,1,0:T(8,128)(2,1)S(1)}, bf16[3,256,128]{2,1,0:T(8,128)(2,1)S(1)}, u32[]{:S(2)}, u32[]{:S(2)}) collective-permute-start(bf16[3,256,128]{2,1,0:T(8,128)(2,1)S(1)} %pad_maximum_fusion.6), channel_id=1, source_target_pairs={{1,0},{2,1},{3,2},{5,4},{6,5},{7,6},{9,8},{10,9},{11,10},{13,12},{... | collective-permute-start | bytes 589832 | tf_op jit(solution)/shard_map/ppermute | solution.py:20
Sparse Core Ops, SparseCore 0:
  92.6 41.1 reduce-scatter.2
  137.1 41.1 reduce-scatter.4
  180.8 38.5 all-reduce.3

commit v2 on v0

v2 whole, which is shorter than its diff:
```python
import functools

import jax
import jax.numpy as jnp
from jax import lax
from jax.experimental import pallas as pl
from jax.experimental.pallas import tpu as pltpu
from jax.sharding import PartitionSpec as P

BLK = 64
UNROLL = 3
GROUPS = 3
F32 = jnp.float32
BF16 = jnp.bfloat16
MESH = pl.DeviceIdType.MESH
DIRECTIONS = ((-1, -1), (-1, 0), (-1, 1), (0, -1), (0, 1), (1, -1), (1, 0), (1, 1))

VM = pl.BlockSpec(memory_space=pltpu.VMEM)
SM = pl.BlockSpec(memory_space=pltpu.SMEM)


def column(table, k):
    lanes = lax.broadcasted_iota(jnp.int32, table.shape, 1)
    return jnp.sum(jnp.where(lanes == k, table, 0.0), axis=1, keepdims=True)


def whole_kernel(
    nx, ny,
    count, send, features, cotangent, rule, hi, lo, w1, w2,
    output, grad_input, grad_one, grad_two,
    table1, table2, field, hidden, upstream, grad, pre, gathered, acc, own1, own2, sums,
    outs, backs, rets, gsend, grecv, ysend, yrecv,
    halo_ss, halo_rs, gss, grs, yss, yrs,
):
    a, b = lax.axis_index("gx"), lax.axis_index("gy")
    nblk, blk, channels = field.shape
    rows = nblk * blk
    half = rows // 2
    kernel = w1.shape[0]
    per = send.shape[1]
    slot = per * blk
    chunk = channels // nx
    span = kernel // GROUPS
    pieces = acc.shape[1] // channels

    def exists(e):
        dx, dy = DIRECTIONS[e]
        x, y = a + dx, b + dy
        return (x >= 0) & (x < nx) & (y >= 0) & (y < ny)

    def place(e):
        dx, dy = DIRECTIONS[e]
        return (a + dx, b + dy)

    def gx_peer(off):
        return (lax.rem(a + off, nx), b)

    def gy_peer(off):
        return (a, lax.rem(b + off, ny))

    table1[...] = jnp.zeros_like(table1)
    table2[...] = jnp.zeros_like(table2)
    rets[...] = jnp.zeros_like(rets)

    barrier = pltpu.get_barrier_semaphore()
    for off in range(1, nx):
        pl.semaphore_signal(barrier, inc=1, device_id=gx_peer(off), device_id_type=MESH)
    for off in range(1, ny):
        pl.semaphore_signal(barrier, inc=1, device_id=gy_peer(off), device_id_type=MESH)
    corners = (0, 2, 5, 7)
    for e in corners:
        dx, dy = DIRECTIONS[e]
        corner = (lax.rem(a + dx + nx, nx), lax.rem(b + dy + ny, ny))
        pl.semaphore_signal(barrier, inc=1, device_id=corner, device_id_type=MESH)

    ids = lax.broadcasted_iota(jnp.int32, (rows, 1), 0)
    live = (ids < count[0, 0] * blk).astype(F32)
    masked = (features[...].astype(F32) * live).astype(BF16)
    field[...] = masked.reshape(nblk, blk, channels)
    upstream[...] = (cotangent[...].astype(F32) * live).astype(BF16)
    table1[:, :channels] = masked

    pl.semaphore_wait(barrier, nx - 1 + ny - 1 + len(corners))

    def slot_view(table, j):
        return table.at[pl.ds((j % 2) * half, half), pl.ds((1 + j // 2) * channels, channels)]

    def ext_copy(x, e, table):
        return pltpu.make_async_remote_copy(
            src_ref=outs.at[x, e], dst_ref=slot_view(table, 7 - e),
            send_sem=halo_ss.at[x, e], recv_sem=halo_rs.at[x, 7 - e],
            device_id=place(e), device_id_type=MESH,
        )

    def back_copy(x, j):
        return pltpu.make_async_remote_copy(
            src_ref=backs.at[x, j], dst_ref=rets.at[x, j],
            send_sem=halo_ss.at[2 + x, j], recv_sem=halo_rs.at[2 + x, j],
            device_id=place(j), device_id_type=MESH,
        )

    def send_ext(x, source, table):
        for e in range(8):
            for s in range(per):
                outs[x, e, s * blk : (s + 1) * blk, :] = source[send[e, s]]

            @pl.when(exists(e))
            def _():
                ext_copy(x, e, table).start()

    def wait_ext(x, table):
        for e in range(8):
            @pl.when(exists(7 - e))
            def _():
                ext_copy(x, e, table).wait_recv()

    def send_back(x):
        for j in range(8):
            base = (j % 2) * half
            col = (1 + j // 2) * channels
            backs[x, j] = acc[base : base + half, col : col + channels].astype(BF16)

            @pl.when(exists(j))
            def _():
                back_copy(x, j).start()

    def wait_back(x):
        for j in range(8):
            @pl.when(exists(7 - j))
            def _():
                back_copy(x, j).wait_recv()

    def returned_total(x, own):
        for n in range(nblk):
            total = own[n * blk : (n + 1) * blk, :]
            for e in range(8):
                for s in range(per):
                    share = jnp.where(send[7 - e, s] == n, 1.0, 0.0)
                    total += share * rets[x, e, s * blk : (s + 1) * blk, :].astype(F32)
            own[n * blk : (n + 1) * blk, :] = total

    def scatter(k, g, w):
        terms = lax.dot_general(g, w[k], (((1,), (1,)), ((), ())), preferred_element_type=F32)
        low = column(lo[...], k)
        wide = jnp.concatenate(
            [jnp.where(low == float(p), terms, 0.0).astype(BF16) for p in range(pieces)], axis=1
        )
        picked = rule[pl.ds(k, 1), :]
        hot = lax.broadcasted_iota(jnp.int32, (rows, rows), 0) == lax.rem(picked, rows)
        hot = jnp.where(hot, 1.0, 0.0).astype(BF16)
        return jnp.dot(hot, wide, preferred_element_type=F32)

    def gather(k, table):
        high, low = column(hi[...], k), column(lo[...], k)
        lanes = lax.broadcasted_iota(jnp.int32, (rows, rows), 1).astype(F32)
        hot = jnp.where(lanes == high, 1.0, 0.0).astype(BF16)
        found = jnp.dot(hot, table[...], preferred_element_type=F32)
        picked = jnp.zeros((rows, channels), F32)
        for p in range(pieces):
            picked = jnp.where(low == float(p), found[:, p * channels : (p + 1) * channels], picked)
        return picked.astype(BF16)

    def run(start, stop, body, into):
        @pl.loop(start // UNROLL, stop // UNROLL)
        def _(step):
            total = None
            for u in range(UNROLL):
                part = body(step * UNROLL + u)
                total = part if total is None else total + part
            into[...] += total

    def keep_partial(t, k, rows_in, rows_out):
        part = lax.dot_general(rows_in, rows_out, (((0,), (0,)), ((), ())), preferred_element_type=F32)
        at = k - (t % GROUPS) * span
        for p in range(nx):
            gsend[t, p, at] = part[p * chunk : (p + 1) * chunk, :].astype(BF16)

    def gx_copy(t, off):
        peer = gx_peer(off)
        return pltpu.make_async_remote_copy(
            src_ref=gsend.at[t, peer[0]], dst_ref=grecv.at[t, off],
            send_sem=gss.at[t, off], recv_sem=grs.at[t, off],
            device_id=peer, device_id_type=MESH,
        )

    def gy_copy(t, off):
        return pltpu.make_async_remote_copy(
            src_ref=ysend.at[t], dst_ref=yrecv.at[t, off],
            send_sem=yss.at[t, off], recv_sem=yrs.at[t, off],
            device_id=gy_peer(off), device_id_type=MESH,
        )

    def reduce_gx(t):
        total = gsend[t, a].astype(F32)
        for off in range(1, nx):
            gx_copy(t, off).wait_recv()
            total += grecv[t, off].astype(F32)
        ysend[t] = total.astype(BF16)
        for off in range(1, ny):
            gy_copy(t, off).start()

    def reduce_gy(t):
        for off in range(1, ny):
            gy_copy(t, off).wait_recv()
        total = jnp.zeros(ysend.shape[1:], F32)
        for source in range(ny):
            term = jnp.where(source == b, ysend[t].astype(F32), 0.0)
            for off in range(1, ny):
                here = lax.rem(b - off + ny, ny) == source
                term = jnp.where(here, yrecv[t, off].astype(F32), term)
            total += term
        out = grad_one if t < GROUPS else grad_two
        first = (t % GROUPS) * span
        out[first : first + span] = total * (1.0 / (nx * ny))

    def after_group(t):
        for off in range(1, nx):
            gx_copy(t, off).start()
        if t >= 1:
            reduce_gx(t - 1)
        if t >= 2:
            reduce_gy(t - 2)

    send_ext(0, field, table1)
    acc[...] = jnp.zeros_like(acc)
    run(0, kernel, lambda k: scatter(k, upstream[...], w2), acc)
    send_back(0)
    own2[...] = acc[:, :channels]

    wait_ext(0, table1)
    pre[...] = jnp.zeros_like(pre)

    def first_conv(k):
        picked = gather(k, table1)
        gathered[k] = picked
        return jnp.dot(picked, w1[k], preferred_element_type=F32)

    run(0, kernel, first_conv, pre)
    v = pre[...] * live
    pre[...] = v
    hid = (v / (1.0 + jnp.exp(-v))).astype(BF16)
    hidden[...] = hid.reshape(nblk, blk, channels)
    table2[:, :channels] = hid
    send_ext(1, hidden, table2)

    wait_back(0)
    returned_total(0, own2)
    v = pre[...]
    s = 1.0 / (1.0 + jnp.exp(-v))
    grad[...] = (own2[...] * s * (1.0 + v * (1.0 - s)) * live).astype(BF16)
    acc[...] = jnp.zeros_like(acc)
    for t in range(GROUPS):
        def second_scatter(k, t=t):
            keep_partial(t, k, gathered[k], grad[...])
            return scatter(k, grad[...], w1)

        run(t * span, (t + 1) * span, second_scatter, acc)
        after_group(t)
    send_back(1)
    own1[...] = acc[:, :channels]

    wait_ext(1, table2)
    sums[...] = jnp.zeros_like(sums)
    for t in range(GROUPS, 2 * GROUPS):
        def second_conv(k, t=t):
            picked = gather(k, table2)
            keep_partial(t, k, picked, upstream[...])
            return jnp.dot(picked, w2[k], preferred_element_type=F32)

        run((t - GROUPS) * span, (t + 1 - GROUPS) * span, second_conv, sums)
        after_group(t)
    output[...] = (sums[...] * live).astype(BF16)
    wait_back(1)
    returned_total(1, own1)
    grad_input[...] = (own1[...] * live).astype(BF16)
    last = 2 * GROUPS - 1
    reduce_gx(last)
    reduce_gy(last - 1)
    reduce_gy(last)

    for e in range(8):
        @pl.when(exists(e))
        def _():
            ext_copy(0, e, table1).wait_send()
            ext_copy(1, e, table2).wait_send()
            back_copy(0, e).wait_send()
            back_copy(1, e).wait_send()
    for t in range(2 * GROUPS):
        for off in range(1, nx):
            gx_copy(t, off).wait_send()
        for off in range(1, ny):
            gy_copy(t, off).wait_send()


def on_device(features, cotangent, weight_one, weight_two, block_count, send_list, rulebook):
    field, cot = features[0, 0], cotangent[0, 0]
    send, rule = send_list[0, 0], rulebook[0, 0]
    rows, channels = field.shape
    kernel = rule.shape[0]
    slot = send.shape[1] * BLK
    nx, ny = lax.axis_size("gx"), lax.axis_size("gy")
    chunk = channels // nx
    span = kernel // GROUPS
    wide = (rows, channels * (1 + 8 * slot // rows))
    columns = jnp.pad(rule.T, ((0, 0), (0, 128 - kernel)))
    hi = (columns % rows).astype(F32)
    lo = (columns // rows).astype(F32)
    shape = jax.ShapeDtypeStruct
    grads = shape((kernel, chunk, channels), F32)
    plain_f = pltpu.VMEM((rows, channels), F32)
    plain_b = pltpu.VMEM((rows, channels), BF16)
    blocks = pltpu.VMEM((rows // BLK, BLK, channels), BF16)
    halos = pltpu.VMEM((2, 8, slot, channels), BF16)
    parts = 2 * GROUPS
    sem = pltpu.SemaphoreType.DMA
    output, grad_input, one, two = pl.pallas_call(
        functools.partial(whole_kernel, nx, ny),
        out_shape=(shape((rows, channels), BF16),) * 2 + (grads, grads),
        in_specs=[SM, SM] + [VM] * 7,
        out_specs=(VM,) * 4,
        scratch_shapes=[
            pltpu.VMEM(wide, BF16), pltpu.VMEM(wide, BF16), blocks, blocks, plain_b, plain_b,
            plain_f, pltpu.VMEM((kernel, rows, channels), BF16), pltpu.VMEM(wide, F32),
            plain_f, plain_f, plain_f, halos, halos, halos,
            pltpu.VMEM((parts, nx, span, chunk, channels), BF16),
            pltpu.VMEM((parts, nx, span, chunk, channels), BF16),
            pltpu.VMEM((parts, span, chunk, channels), BF16),
            pltpu.VMEM((parts, ny, span, chunk, channels), BF16),
            sem((4, 8)), sem((4, 8)), sem((parts, nx)), sem((parts, nx)),
            sem((parts, ny)), sem((parts, ny)),
        ],
        compiler_params=pltpu.CompilerParams(
            vmem_limit_bytes=56 << 20, collective_id=0, has_side_effects=True
        ),
    )(block_count, send, field, cot, rule, hi, lo, weight_one, weight_two)
    return output[None, None], grad_input[None, None], one, two


def solution(mesh):
    placed = (
        P("gx", "gy", None, None),
        P("gx", "gy", None, None),
        P(),
        P(),
        P("gx", "gy"),
        P("gx", "gy", None, None),
        P("gx", "gy", None, None),
    )
    return jax.shard_map(
        on_device,
        mesh=mesh,
        in_specs=placed,
        out_specs=(
            P("gx", "gy", None, None),
            P("gx", "gy", None, None),
            P(None, "gx", None),
            P(None, "gx", None),
        ),
        check_vma=False,
    )
```

time: 523 us -> 101 us (0.19)
  other arithmetic: 160 us -> 1.05 us
  starting transfers between devices: 143 us -> 0 us
  local copies, waits for them, and re-layouts: 119 us -> 6.98 us
  Pallas kernels: 0 us -> 91.5 us
  waiting for transfers between devices: 56.7 us -> 0 us
  matrix products: 25.6 us -> 0 us
  between operations: 15.6 us -> 1.32 us
    scatter-add x4 -> x0, other arithmetic: 153 us -> none  [the longest x2 149 us: conv_add_block(): return (totals.at[indices.reshape(-1)].add(terms), None)]
    ppermute x48 -> x0, starting transfers between devices: 143 us -> none  [shifted(): return lax.ppermute(block, axis, route)]
    pallas_call x0 -> x1, Pallas kernels: none -> 91.5 us  [on_device(): pl.pallas_call(functools.partial(whole_kernel, nx, ny), out_shape=(shape(...]
    gather x6 -> x0, local copies, waits for them, and re-layouts: 71.4 us -> none  [the longest x4 70.1 us: one_block(): gathered = extended[indices].reshape(block_span, kernel * channels)]
    reshape x6 -> x0, local copies, waits for them, and re-layouts: 31.3 us -> none  [the longest x2 15.9 us: conv_add_block(): jnp.dot(pieces, flipped, preferred_element_type=jnp.float32)]
    ppermute x48 -> x0, waiting for transfers between devices: 28.6 us -> none  [shifted(): return lax.ppermute(block, axis, route)]
    psum x1 -> x0, waiting for transfers between devices: 28 us -> none  [on_device(): summed_one, summed_two = lax.psum((slab_one, slab_two), 'gy')]
    dot_general x6 -> x0, matrix products: 25.6 us -> none  [the longest x2 9.36 us: conv_add_block(): jnp.dot(pieces, flipped, preferred_element_type=jnp.float32)]
  transfers between devices with their start and end apart: 51 -> 0, of which waited for: 14 -> 0; matrix products, arithmetic and copies ran while one was open for 33% -> 0% of each run, Pallas kernels for 0% -> 0%
where the time goes in v2:
time: 101 us
  Pallas kernels  91.5 us (91%)
  local copies, waits for them, and re-layouts  6.98 us (7%)
  between operations  1.32 us (1%)
  other arithmetic  1.05 us (1%)
    pallas_call x1, Pallas kernels, on_device(): pl.pallas_call(functools.partial(whole_kernel, nx, ny), out_shape=(shape(...  91.5 us
    unnamed x15, local copies, waits for them, and re-layouts  4.79 us
    squeeze x2, local copies, waits for them, and re-layouts, on_device(): send, rule = (send_list[0, 0], rulebook[0, 0])  2.19 us

profile of v2, /device:TPU:0, one launch (start us, length us, event | category | flops | bytes accessed | tf_op | source)
XLA Modules:
  0.0 100.9 jit_solution(4486906536887169967)
XLA Ops:
  1.3 0.0 copy-start.4
  1.3 0.7 copy-done.4
  2.0 0.7 copy.12.send
  2.6 0.0 copy-start.2
  2.6 1.5 %copy.16 = s32[1,1,27,512]{3,2,0,1:T(8,128)} copy(s32[1,1,27,512]{3,1,2,0:T(1,128)} %param.13) | data formatting | bytes 110592 | tf_op jit(solution)/shard_map/squeeze | solution.py:297
  4.2 0.0 copy-done.2
  4.2 0.1 copy.11
  4.3 1.1 %fusion.1 = (f32[512,128]{1,0:T(8,128)}, f32[512,128]{1,0:T(8,128)}) fusion(s32[512,27]{1,0:T(8,128)S(1)} %bitcast.11), kind=kLoop, calls=%fused_computation.6 | loop fusion | flops 1376256 | bytes 579584 | tf_op jit(solution)/shard_map/convert_element_type | solution.py:307
  5.4 91.5 %shard_map.102 = (bf16[512,128]{1,0:T(8,128)(2,1)}, bf16[512,128]{1,0:T(8,128)(2,1)}, f32[27,16,128]{2,1,0:T(8,128)}, f32[27,16,128]{2,1,0:T(8,128)}) custom-call(s32[1,1]{1,0:T(1,128)S(6)} %copy.21.count, s32[8,4]{1,0:T(8,128)} %copy.12.send, bf16[512,128]{1,0:T(8,128)(2,1)} %bitcast.13, bf16[512,128]{1,0:T(8,128)(2,1)} %bitcast.14, s32[27,512]{1,0:T(8,128)} %bitcast.12, ...), custom_call_target="tpu_custom_call" | custom-call | tf_op jit(solution)/shard_map/pallas_call | solution.py:316
  96.9 0.0 copy-start.3
  96.9 0.0 copy-start.1
  96.9 1.6 %copy.22 = bf16[1,1,512,128]{3,2,1,0:T(8,128)(2,1)} copy(bf16[1,1,512,128]{3,2,1,0:T(8,128)(2,1)} %bitcast.16) | data formatting | bytes 262144
  98.5 0.0 copy-done.3
  98.5 0.7 copy.23
  99.2 0.0 copy-done.1
  99.2 0.0 copy-start
  99.2 0.7 copy.24
  99.9 0.3 copy-done
  100.2 0.7 copy.25
Async XLA Ops:
  1.3 0.7 copy-start.4
  2.6 1.5 %copy-start.2 = (s32[1,1,27,512]{3,1,2,0:T(1,128)S(1)}, s32[1,1,27,512]{3,1,2,0:T(1,128)}, u32[]{:S(2)}) copy-start(s32[1,1,27,512]{3,1,2,0:T(1,128)} %param.13) | copy-start | bytes 165892
  96.9 1.6 %copy-start.3 = (bf16[512,128]{1,0:T(8,128)(2,1)S(1)}, bf16[512,128]{1,0:T(8,128)(2,1)}, u32[]{:S(2)}) copy-start(bf16[512,128]{1,0:T(8,128)(2,1)} %get-tuple-element.9) | copy-start | bytes 393220
  96.9 2.3 %copy-start.1 = (f32[27,16,128]{2,1,0:T(8,128)S(1)}, f32[27,16,128]{2,1,0:T(8,128)}, u32[]{:S(2)}) copy-start(f32[27,16,128]{2,1,0:T(8,128)} %get-tuple-element.20) | copy-start | bytes 663556
  99.2 1.0 %copy-start = (f32[27,16,128]{2,1,0:T(8,128)S(1)}, f32[27,16,128]{2,1,0:T(8,128)}, u32[]{:S(2)}) copy-start(f32[27,16,128]{2,1,0:T(8,128)} %get-tuple-element.21) | copy-start | bytes 663556

commit v3 on v2

--- a/solution.py
+++ b/solution.py
@@ -139,16 +139,26 @@
                     total += share * rets[x, e, s * blk : (s + 1) * blk, :].astype(F32)
             own[n * blk : (n + 1) * blk, :] = total
 
-    def scatter(k, g, w):
-        terms = lax.dot_general(g, w[k], (((1,), (1,)), ((), ())), preferred_element_type=F32)
-        low = column(lo[...], k)
-        wide = jnp.concatenate(
-            [jnp.where(low == float(p), terms, 0.0).astype(BF16) for p in range(pieces)], axis=1
-        )
-        picked = rule[pl.ds(k, 1), :]
-        hot = lax.broadcasted_iota(jnp.int32, (rows, rows), 0) == lax.rem(picked, rows)
-        hot = jnp.where(hot, 1.0, 0.0).astype(BF16)
-        return jnp.dot(hot, wide, preferred_element_type=F32)
+    def stacked(w, ks):
+        return w[pl.ds(ks[0], UNROLL)].reshape(UNROLL * channels, channels)
+
+    def scatter(ks, g, w):
+        terms = lax.dot_general(
+            g, stacked(w, ks), (((1,), (1,)), ((), ())), preferred_element_type=F32
+        )
+        tall, hots = [], []
+        for u, k in enumerate(ks):
+            low = column(lo[...], k)
+            term = terms[:, u * channels : (u + 1) * channels]
+            tall.append(jnp.concatenate(
+                [jnp.where(low == float(p), term, 0.0).astype(BF16) for p in range(pieces)], axis=1
+            ))
+            picked = rule[pl.ds(k, 1), :]
+            hot = lax.broadcasted_iota(jnp.int32, (rows, rows), 0) == lax.rem(picked, rows)
+            hots.append(jnp.where(hot, 1.0, 0.0).astype(BF16))
+        return jnp.dot(
+            jnp.concatenate(hots, axis=1), jnp.concatenate(tall, axis=0), preferred_element_type=F32
+        )
 
     def gather(k, table):
         high, low = column(hi[...], k), column(lo[...], k)
@@ -163,17 +173,15 @@
     def run(start, stop, body, into):
         @pl.loop(start // UNROLL, stop // UNROLL)
         def _(step):
-            total = None
-            for u in range(UNROLL):
-                part = body(step * UNROLL + u)
-                total = part if total is None else total + part
-            into[...] += total
-
-    def keep_partial(t, k, rows_in, rows_out):
+            into[...] += body([step * UNROLL + u for u in range(UNROLL)])
+
+    def keep_partial(t, ks, rows_in, rows_out):
         part = lax.dot_general(rows_in, rows_out, (((0,), (0,)), ((), ())), preferred_element_type=F32)
-        at = k - (t % GROUPS) * span
-        for p in range(nx):
-            gsend[t, p, at] = part[p * chunk : (p + 1) * chunk, :].astype(BF16)
+        for u, k in enumerate(ks):
+            at = k - (t % GROUPS) * span
+            for p in range(nx):
+                first = u * channels + p * chunk
+                gsend[t, p, at] = part[first : first + chunk, :].astype(BF16)
 
     def gx_copy(t, off):
         peer = gx_peer(off)
@@ -223,17 +231,20 @@
 
     send_ext(0, field, table1)
     acc[...] = jnp.zeros_like(acc)
-    run(0, kernel, lambda k: scatter(k, upstream[...], w2), acc)
+    run(0, kernel, lambda ks: scatter(ks, upstream[...], w2), acc)
     send_back(0)
     own2[...] = acc[:, :channels]
 
     wait_ext(0, table1)
     pre[...] = jnp.zeros_like(pre)
 
-    def first_conv(k):
-        picked = gather(k, table1)
-        gathered[k] = picked
-        return jnp.dot(picked, w1[k], preferred_element_type=F32)
+    def first_conv(ks):
+        picks = [gather(k, table1) for k in ks]
+        for k, picked in zip(ks, picks):
+            gathered[k] = picked
+        return jnp.dot(
+            jnp.concatenate(picks, axis=1), stacked(w1, ks), preferred_element_type=F32
+        )
 
     run(0, kernel, first_conv, pre)
     v = pre[...] * live
@@ -250,9 +261,10 @@
     grad[...] = (own2[...] * s * (1.0 + v * (1.0 - s)) * live).astype(BF16)
     acc[...] = jnp.zeros_like(acc)
     for t in range(GROUPS):
-        def second_scatter(k, t=t):
-            keep_partial(t, k, gathered[k], grad[...])
-            return scatter(k, grad[...], w1)
+        def second_scatter(ks, t=t):
+            picks = jnp.concatenate([gathered[k] for k in ks], axis=1)
+            keep_partial(t, ks, picks, grad[...])
+            return scatter(ks, grad[...], w1)
 
         run(t * span, (t + 1) * span, second_scatter, acc)
         after_group(t)
@@ -262,10 +274,10 @@
     wait_ext(1, table2)
     sums[...] = jnp.zeros_like(sums)
     for t in range(GROUPS, 2 * GROUPS):
-        def second_conv(k, t=t):
-            picked = gather(k, table2)
-            keep_partial(t, k, picked, upstream[...])
-            return jnp.dot(picked, w2[k], preferred_element_type=F32)
+        def second_conv(ks, t=t):
+            picks = jnp.concatenate([gather(k, table2) for k in ks], axis=1)
+            keep_partial(t, ks, picks, upstream[...])
+            return jnp.dot(picks, stacked(w2, ks), preferred_element_type=F32)
 
         run((t - GROUPS) * span, (t + 1 - GROUPS) * span, second_conv, sums)
         after_group(t)

time: 101 us -> 94.7 us (0.938)
  Pallas kernels: 91.5 us -> 85.1 us
    pallas_call x1, Pallas kernels: 91.5 us -> 85.1 us  [on_device(): pl.pallas_call(functools.partial(whole_kernel, nx, ny), out_shape=(shape(...]
where the time goes in v3:
time: 94.7 us; the launch traced here: 94.5 us
  Pallas kernels  85.1 us (90%)
  local copies, waits for them, and re-layouts  6.98 us (7%)
  between operations  1.32 us (1%)
  other arithmetic  1.05 us (1%)
    pallas_call x1, Pallas kernels, on_device(): pl.pallas_call(functools.partial(whole_kernel, nx, ny), out_shape=(shape(...  85.1 us
    unnamed x15, local copies, waits for them, and re-layouts  4.79 us
    squeeze x2, local copies, waits for them, and re-layouts, on_device(): send, rule = (send_list[0, 0], rulebook[0, 0])  2.19 us

profile of v3, /device:TPU:0, one launch (start us, length us, event | category | flops | bytes accessed | tf_op | source)
XLA Modules:
  0.0 94.5 jit_solution(3052458149283667157)
XLA Ops:
  1.3 0.0 copy-start.4
  1.3 0.7 copy-done.4
  2.0 0.7 copy.12.send
  2.6 0.0 copy-start.2
  2.6 1.5 %copy.16 = s32[1,1,27,512]{3,2,0,1:T(8,128)} copy(s32[1,1,27,512]{3,1,2,0:T(1,128)} %param.13) | data formatting | bytes 110592 | tf_op jit(solution)/shard_map/squeeze | solution.py:309
  4.2 0.0 copy-done.2
  4.2 0.1 copy.11
  4.3 1.1 %fusion.1 = (f32[512,128]{1,0:T(8,128)}, f32[512,128]{1,0:T(8,128)}) fusion(s32[512,27]{1,0:T(8,128)S(1)} %bitcast.11), kind=kLoop, calls=%fused_computation.6 | loop fusion | flops 1376256 | bytes 579584 | tf_op jit(solution)/shard_map/convert_element_type | solution.py:319
  5.4 85.1 %shard_map.102 = (bf16[512,128]{1,0:T(8,128)(2,1)}, bf16[512,128]{1,0:T(8,128)(2,1)}, f32[27,16,128]{2,1,0:T(8,128)}, f32[27,16,128]{2,1,0:T(8,128)}) custom-call(s32[1,1]{1,0:T(1,128)S(6)} %copy.21.count, s32[8,4]{1,0:T(8,128)} %copy.12.send, bf16[512,128]{1,0:T(8,128)(2,1)} %bitcast.13, bf16[512,128]{1,0:T(8,128)(2,1)} %bitcast.14, s32[27,512]{1,0:T(8,128)} %bitcast.12, ...), custom_call_target="tpu_custom_call" | custom-call | tf_op jit(solution)/shard_map/pallas_call | solution.py:328
  90.5 0.0 copy-start.3
  90.5 0.0 copy-start.1
  90.5 1.6 %copy.22 = bf16[1,1,512,128]{3,2,1,0:T(8,128)(2,1)} copy(bf16[1,1,512,128]{3,2,1,0:T(8,128)(2,1)} %bitcast.16) | data formatting | bytes 262144
  92.1 0.0 copy-done.3
  92.1 0.7 copy.23
  92.8 0.0 copy-done.1
  92.8 0.0 copy-start
  92.8 0.7 copy.24
  93.4 0.3 copy-done
  93.8 0.7 copy.25
Async XLA Ops:
  1.3 0.7 copy-start.4
  2.6 1.5 %copy-start.2 = (s32[1,1,27,512]{3,1,2,0:T(1,128)S(1)}, s32[1,1,27,512]{3,1,2,0:T(1,128)}, u32[]{:S(2)}) copy-start(s32[1,1,27,512]{3,1,2,0:T(1,128)} %param.13) | copy-start | bytes 165892
  90.5 1.6 %copy-start.3 = (bf16[512,128]{1,0:T(8,128)(2,1)S(1)}, bf16[512,128]{1,0:T(8,128)(2,1)}, u32[]{:S(2)}) copy-start(bf16[512,128]{1,0:T(8,128)(2,1)} %get-tuple-element.9) | copy-start | bytes 393220
  90.5 2.3 %copy-start.1 = (f32[27,16,128]{2,1,0:T(8,128)S(1)}, f32[27,16,128]{2,1,0:T(8,128)}, u32[]{:S(2)}) copy-start(f32[27,16,128]{2,1,0:T(8,128)} %get-tuple-element.20) | copy-start | bytes 663556
  92.8 1.0 %copy-start = (f32[27,16,128]{2,1,0:T(8,128)S(1)}, f32[27,16,128]{2,1,0:T(8,128)}, u32[]{:S(2)}) copy-start(f32[27,16,128]{2,1,0:T(8,128)} %get-tuple-element.21) | copy-start | bytes 663556
